TPU v7x, 32 devices: a whole 2x2x4 slice. The times are simulated.
32 devices in a mesh: groups: 2 (over y), ctx: 4 (over z), head: 4 (over x, core).
Axes of the slice: x: 2, y: 2, z: 4, core: 2. Of those that a mesh axis runs over, the one named last changes fastest.
Arguments:
- queries: bfloat16 [64, 2048, 128], P(('groups', 'head'), 'ctx'), parts along dimension 0, may hold values from -48 to 48
- key_rows: bfloat16 [8, 2048, 128], P(('groups', 'head'), 'ctx'), parts along dimension 0, may hold values from -6 to 6
- value_rows: bfloat16 [8, 2048, 128], P(('groups', 'head'), 'ctx'), parts along dimension 0, may hold values from -6 to 6
- out_grad: bfloat16 [64, 2048, 128], P(('groups', 'head'), 'ctx'), parts along dimension 0, may hold values from -6 to 6
- link_mask: int32 [32, 11], P(('groups', 'ctx')), parts along dimension 0, may hold values from 0 to 1, as said below
Outputs:
- output: bfloat16 [64, 2048, 128], P(('groups', 'head'), 'ctx'), parts along dimension 0
- query_grad: bfloat16 [64, 2048, 128], P(('groups', 'head'), 'ctx'), parts along dimension 0
- key_grad: bfloat16 [8, 2048, 128], P(('groups', 'head'), 'ctx'), parts along dimension 0
- value_grad: bfloat16 [8, 2048, 128], P(('groups', 'head'), 'ctx'), parts along dimension 0
There are 2 independent parts, one for each index of `groups`. A program takes and returns all parts, laid end to end along the dimension named above; each array names one. Nothing has to cross between parts.
Inputs may be any that keep to these rules, and one draw needn't show every extreme that they name: `link_mask`: column 0 is 1 in every row.
All inputs are finite; a program needn't handle non-finite values.
Results may differ from a plain program's by a relative error of at most 0.028.
Values may be sent and summed in bfloat16 or wider, within the bound.
No kernel may reach another device: no remote copies, remote signals or barrier semaphores. Data moves between devices by JAX's collectives and lax.ppermute only.
A program may use at most 64 MiB of HBM per device.

v0:
```python
import functools
import math

import jax
import jax.numpy as jnp
from jax import lax
from jax.experimental import pallas as pl
from jax.experimental.pallas import tpu as pltpu
from jax.sharding import PartitionSpec as P


BLK = 128
NOFF = 11
WIDE = 8
FAR_WIDE = 8
BACK_WIDE = 2
NEG = -1e30
LOG2E = 1.4426950408889634
F32 = jnp.float32
BF16 = jnp.bfloat16


def shift(value, axis, steps, holders):
    count = lax.axis_size(axis)
    return lax.ppermute(value, axis, [(n, n + steps) for n in range(holders, count) if 0 <= n + steps < count])


def slot_table(block_count, ctx_size):
    entries = []
    for slot_id in range(NOFF):
        offset = 0 if slot_id == 0 else 2 ** (slot_id - 1)
        if offset < block_count:
            entries.append((slot_id, offset, 0))
        elif offset // block_count < ctx_size:
            entries.append((slot_id, offset, offset // block_count))
    return entries


def dot_nt(a, b):
    return lax.dot_general(a, b, (((1,), (1,)), ((), ())), preferred_element_type=F32)


def dot_nn(a, b):
    return lax.dot_general(a, b, (((1,), (0,)), ((), ())), preferred_element_type=F32)


def block(n):
    return slice(n * BLK, (n + 1) * BLK)


def stack(parts, axis=0):
    return parts[0] if len(parts) == 1 else jnp.concatenate(parts, axis=axis)


class Plan:
    def __init__(self, blocks, heads, size, ctx_size):
        self.blocks, self.heads, self.size = blocks, heads, size
        self.entries = slot_table(blocks, ctx_size)
        self.lanes = heads * BLK
        near = [(n, e[1]) for n, e in enumerate(self.entries) if e[1] <= blocks]
        self.far = [n for n, e in enumerate(self.entries) if e[1] > blocks]
        self.hops = [self.entries[n][2] for n in self.far]
        self.own = [[(n, i - o) for n, o in near if o <= i] for i in range(blocks)]
        self.prev = [[(n, i - o + blocks) for n, o in near if o > i] for i in range(blocks)]
        self.own_at = [sum(len(s) for s in self.own[:i]) for i in range(blocks + 1)]
        self.prev_at = [sum(len(s) for s in self.prev[:i]) for i in range(blocks + 1)]
        self.scale = LOG2E / math.sqrt(size)
        self.inv_root = 1.0 / math.sqrt(size)

    def chunks(self, wide):
        for first in range(0, self.heads, wide):
            yield slice(first, first + wide), slice(first * BLK, (first + wide) * BLK)

    def items(self, wide, rows=None):
        for i in range(self.blocks) if rows is None else rows:
            for heads, lanes in self.chunks(wide):
                yield i, heads, lanes


def rows_of(ref, heads, i, size):
    return ref[heads, block(i)].reshape(-1, size)


def with_ones(values_t):
    width = values_t.shape[1]
    row = lax.broadcasted_iota(jnp.int32, (16, width), 0)
    return jnp.concatenate([values_t, jnp.where(row == 0, 1.0, 0.0).astype(BF16)], axis=0)


def scores_of(plan, raw, biases, mask, top):
    parts = [raw[block(n)] for n in range(len(biases))]
    if mask is not None:
        parts[0] = parts[0] + mask
    for part, bias in zip(parts, biases):
        high = jnp.max(part, axis=0, keepdims=True) * plan.scale
        if bias is not None:
            high = high + bias
        top = high if top is None else jnp.maximum(top, high)
    exps = []
    for part, bias in zip(parts, biases):
        base = top if bias is None else top - bias
        exps.append(jnp.exp2(part * plan.scale - base))
    return exps, top


def staged(items, first, second):
    items = list(items)
    ahead = first(items[0])
    for n, item in enumerate(items):
        now = ahead
        if n + 1 < len(items):
            ahead = first(items[n + 1])
        second(item, now)


def causal_mask(plan, mask_ref):
    key = lax.broadcasted_iota(jnp.int32, mask_ref.shape, 0)
    row = lax.broadcasted_iota(jnp.int32, mask_ref.shape, 1)
    mask_ref[...] = jnp.where(key <= lax.rem(row, BLK), 0.0, NEG)


def local_forward(
    plan, link_ref, causal_ref, q_ref, do_ref, k_ref, v_ref, bias_ref, stat_ref, acc_ref, p_ref, dot_ref
):
    first_block = lax.axis_index("ctx") * plan.blocks
    scalars = []
    for i in range(plan.blocks):
        scalars.append([])
        for n, (slot_id, offset, _) in enumerate(plan.entries):
            live = (link_ref[i, slot_id] == 1) & (first_block + i >= offset)
            scalars[i].append(jnp.where(live, 0.0, NEG).astype(F32))
            bias_ref[i, n : n + 1, :] = jnp.full((1, plan.lanes), scalars[i][n], F32)
    values_t = with_ones(v_ref[0].T)
    size = plan.size

    def first(item):
        i, heads, _ = item
        keys = stack([k_ref[0, block(b)] for _, b in plan.own[i]])
        return dot_nt(keys, rows_of(q_ref, heads, i, size))

    def second(item, raw):
        i, heads, lanes = item
        slots = plan.own[i]
        vt = stack([values_t[:, block(b)] for _, b in slots], axis=1)
        biases = [scalars[i][n] if plan.entries[n][1] > 0 else None for n, _ in slots]
        at = plan.own_at[i] * BLK
        exps, top = scores_of(plan, raw, biases, causal_ref[:, lanes], None)
        low = stack([part.astype(BF16) for part in exps])
        p_ref[at : at + low.shape[0], lanes] = low
        stat_ref[i, 0:1, lanes] = top
        acc_ref[i, :, lanes] = dot_nn(vt, low)[: size + 8]
        dot_ref[i, :, lanes] = rows_of(do_ref, heads, i, size).T

    staged(plan.items(WIDE), first, second)


def prev_forward(plan, q_ref, k_ref, v_ref, dot_ref, bias_ref, stat_in, acc_in, stat_ref, acc_ref, p_ref):
    size = plan.size
    values_t = with_ones(v_ref[...].T)

    def first(item):
        i, heads, _ = item
        keys = stack([k_ref[block(b)] for _, b in plan.prev[i]])
        return dot_nt(keys, rows_of(q_ref, heads, i, size))

    def second(item, raw):
        i, _, lanes = item
        slots = plan.prev[i]
        vt = stack([values_t[:, block(b)] for _, b in slots], axis=1)
        at = plan.prev_at[i] * BLK
        before = stat_in[i, 0:1, lanes]
        biases = [bias_ref[i, n : n + 1, lanes] for n, _ in slots]
        exps, top = scores_of(plan, raw, biases, None, before)
        low = stack([part.astype(BF16) for part in exps])
        p_ref[at : at + low.shape[0], lanes] = low
        acc = acc_in[i, :, lanes] * jnp.exp2(before - top) + dot_nn(vt, low)[: size + 8]
        acc_ref[i, :, lanes] = acc
        stat_ref[i, 0:1, lanes] = before
        stat_ref[i, 1:2, lanes] = top
        stat_ref[i, 2:3, lanes] = jnp.sum(acc[:size] * dot_ref[i, :, lanes].astype(F32), axis=0, keepdims=True)

    staged(plan.items(WIDE), first, second)


def far_scores(plan, q_ref, dot_ref, k_ref, bias_ref, stat_ref, acc_ref, dv_ref, low_ref, fin_ref):
    size = plan.size
    count = len(plan.far)

    def first(item):
        i, heads, _ = item
        keys = stack([k_ref[f, block(i)] for f in range(count)])
        return dot_nt(keys, rows_of(q_ref, heads, i, size))

    def second(item, raw):
        i, _, lanes = item
        before = stat_ref[i, 1:2, lanes]
        biases = [bias_ref[i, n : n + 1, lanes] for n in plan.far]
        exps, top = scores_of(plan, raw, biases, None, before)
        fade = jnp.exp2(before - top)
        total = acc_ref[i, size : size + 1, lanes] * fade
        total = total + sum(jnp.sum(part, axis=0, keepdims=True) for part in exps)
        inverse = 1.0 / total
        low_ref[i, :, lanes] = (stack(exps) * inverse).astype(BF16)
        fin_ref[i, 0:1, lanes] = jnp.exp2(stat_ref[i, 0:1, lanes] - top) * inverse
        fin_ref[i, 1:2, lanes] = fade * inverse
        fin_ref[i, 2:3, lanes] = stat_ref[i, 2:3, lanes] * (fade * inverse)
        if lanes.stop == plan.lanes:
            dv = dot_nt(low_ref[i], dot_ref[i])
            for f in range(count):
                dv_ref[f, block(i)] = dv[block(f)].astype(BF16)

    staged(plan.items(FAR_WIDE), first, second)


def far_keys(plan, q_ref, dot_ref, v_ref, low_ref, fin_in, dk_ref, ds_ref, fin_ref):
    size = plan.size
    count = len(plan.far)

    def first(item):
        i, _, lanes = item
        values = stack([v_ref[f, block(i)] for f in range(count)])
        return dot_nn(values, dot_ref[i, :, lanes])

    def second(item, grad_w):
        i, _, lanes = item
        weights = low_ref[i, :, lanes].astype(F32)
        products = weights * grad_w
        row_dot = fin_in[i, 2:3, lanes] + jnp.sum(products, axis=0, keepdims=True)
        ds_ref[i, :, lanes] = (products - weights * row_dot).astype(BF16)
        fin_ref[i, 0:2, lanes] = fin_in[i, 0:2, lanes]
        fin_ref[i, 2:3, lanes] = row_dot
        if lanes.stop == plan.lanes:
            dk = dot_nn(ds_ref[i], rows_of(q_ref, slice(0, plan.heads), i, size)) * plan.inv_root
            for f in range(count):
                dk_ref[f, block(i)] = dk[block(f)].astype(BF16)

    staged(plan.items(FAR_WIDE), first, second)


def add_blocks(sums, slots, parts):
    for n, (_, b) in enumerate(slots):
        part = parts[block(n)]
        sums[b] = part if b not in sums else sums[b] + part


def scale_rows(plan, i, factor, dot_ref, fin_ref, scaled_ref):
    for heads, lanes in plan.chunks(BACK_WIDE):
        fade = fin_ref[i, factor : factor + 1, lanes]
        scaled_ref[i, :, lanes] = (dot_ref[i, :, lanes].astype(F32) * fade).astype(BF16)


def score_grads(plan, i, slots, values, factor, fin_ref, p_ref, p_at, ds_ref, ds_at, scaled_ref):
    tall = len(slots) * BLK
    for heads, lanes in plan.chunks(BACK_WIDE):
        fade = fin_ref[i, factor : factor + 1, lanes]
        shifted = dot_nn(values, scaled_ref[i, :, lanes]) - fin_ref[i, 2:3, lanes] * fade
        ds_ref[ds_at : ds_at + tall, lanes] = (p_ref[p_at : p_at + tall, lanes].astype(F32) * shifted).astype(BF16)


def prev_values(plan, dot_ref, fin_ref, p_ref, dv_ref, scaled_ref):
    sums = {}
    for i in range(plan.blocks):
        scale_rows(plan, i, 1, dot_ref, fin_ref, scaled_ref)
        part = p_ref[plan.prev_at[i] * BLK : plan.prev_at[i + 1] * BLK, :]
        add_blocks(sums, plan.prev[i], dot_nt(part, scaled_ref[i]))
    for b in range(plan.blocks):
        dv_ref[block(b)] = sums[b]


def prev_keys(plan, q_ref, v_ref, fin_ref, p_ref, scaled_ref, dk_ref, ds_ref):
    sums = {}
    for i in range(plan.blocks):
        slots = plan.prev[i]
        values = stack([v_ref[block(b)] for _, b in slots])
        at, end = plan.prev_at[i] * BLK, plan.prev_at[i + 1] * BLK
        score_grads(plan, i, slots, values, 1, fin_ref, p_ref, at, ds_ref, at, scaled_ref)
        dk = dot_nn(ds_ref[at:end, :], rows_of(q_ref, slice(0, plan.heads), i, plan.size))
        add_blocks(sums, slots, dk)
    for b in range(plan.blocks):
        dk_ref[block(b)] = sums[b] * plan.inv_root


def local_backward(
    plan, q_ref, dot_ref, k_ref, v_ref, kp_ref, kf_ref, vf_ref, fin_ref, acc_ref, low_ref, p_ref, dsp_ref, dsf_ref,
    dk_ref, dv_ref, o_hbm, dq_hbm, scaled_ref, ds_ref, o_ref, dq_ref, sems,
):
    size = plan.size
    count = len(plan.far)
    copies = []

    def send(source, target, i):
        copies.append(pltpu.make_async_copy(source.at[:, block(i)], target.at[:, block(i)], sems.at[len(copies)]))
        copies[-1].start()

    for i in range(plan.blocks):
        vt = stack([vf_ref[f, block(i)] for f in range(count)]).T
        for heads, lanes in plan.chunks(BACK_WIDE):
            out_t = acc_ref[i, :size, lanes] * fin_ref[i, 1:2, lanes] + dot_nn(vt, low_ref[i, :, lanes])
            o_ref[heads, block(i)] = out_t.astype(BF16).T.reshape(BACK_WIDE, BLK, size)
        send(o_ref, o_hbm, i)
    dk_sums, dv_sums = {}, {}
    keys_t = k_ref[...].T
    prev_t = kp_ref[...].T
    for i in range(plan.blocks):
        slots = plan.own[i]
        values = stack([v_ref[block(b)] for _, b in slots])
        at, end = plan.own_at[i] * BLK, plan.own_at[i + 1] * BLK
        scale_rows(plan, i, 0, dot_ref, fin_ref, scaled_ref)
        score_grads(plan, i, slots, values, 0, fin_ref, p_ref, at, ds_ref, at, scaled_ref)
        kt = [keys_t[:, block(b)] for _, b in slots]
        kt += [prev_t[:, block(b)] for _, b in plan.prev[i]]
        kt += [kf_ref[f, block(i)].T for f in range(count)]
        kt = stack(kt, axis=1)
        for heads, lanes in plan.chunks(BACK_WIDE):
            ds = [ds_ref[at:end, lanes]]
            if plan.prev[i]:
                ds.append(dsp_ref[plan.prev_at[i] * BLK : plan.prev_at[i + 1] * BLK, lanes])
            if count:
                ds.append(dsf_ref[i, :, lanes])
            dq_t = (dot_nn(kt, stack(ds)) * plan.inv_root).astype(BF16)
            dq_ref[heads, block(i)] = dq_t.T.reshape(BACK_WIDE, BLK, size)
        send(dq_ref, dq_hbm, i)
        add_blocks(dv_sums, slots, dot_nt(p_ref[at:end, :], scaled_ref[i]))
        add_blocks(dk_sums, slots, dot_nn(ds_ref[at:end, :], rows_of(q_ref, slice(0, plan.heads), i, size)))
    for b in range(plan.blocks):
        dk_ref[block(b)] = dk_sums[b] * plan.inv_root
        dv_ref[block(b)] = dv_sums[b]
    for copy in copies:
        copy.wait()


def local(queries, key_rows, value_rows, out_grad, link_mask):
    heads, rows, size = queries.shape
    blocks = rows // BLK
    plan = Plan(blocks, heads, size, lax.axis_size("ctx"))
    lanes = plan.lanes
    count = len(plan.far)

    keys, values = key_rows[0], value_rows[0]
    k_prev = shift(keys, "ctx", 1, 0)
    v_prev = shift(values, "ctx", 1, 0)
    k_far, v_far = [], []
    k_last, v_last, at = k_prev, v_prev, 1
    for hop in plan.hops:
        k_last = shift(k_last, "ctx", hop - at, at)
        v_last = shift(v_last, "ctx", hop - at, at)
        at = hop
        k_far.append(k_last)
        v_far.append(v_last)
    if count == 1:
        k_far, v_far = k_far[0][None], v_far[0][None]
    else:
        k_far, v_far = jnp.stack(k_far), jnp.stack(v_far)

    def array(*shape, dtype=BF16):
        return jax.ShapeDtypeStruct(shape, dtype)

    vmem = pl.BlockSpec(memory_space=pltpu.VMEM)
    smem = pl.BlockSpec(memory_space=pltpu.SMEM)
    hbm = pl.BlockSpec(memory_space=pltpu.HBM)

    def call(body, slots, matmuls, outs, operands, scratch=(), places=None, lasts=(), alias=None):
        flops = 2 * matmuls * slots * BLK * lanes * size
        return pl.pallas_call(
            functools.partial(body, plan),
            in_specs=places or [vmem] * len(operands),
            out_specs=[vmem] * (len(outs) - len(lasts)) + list(lasts),
            out_shape=outs,
            scratch_shapes=list(scratch),
            input_output_aliases=alias or {},
            compiler_params=pltpu.CompilerParams(vmem_limit_bytes=20 << 20),
            cost_estimate=pl.CostEstimate(
                flops=flops, bytes_accessed=4 * queries.size, transcendentals=slots * BLK * lanes
            ),
        )(*operands)

    n_own, n_prev, n_far = plan.own_at[-1], plan.prev_at[-1], count * blocks
    stat = array(blocks, 8, lanes, dtype=F32)
    acc = array(blocks, size + 8, lanes, dtype=F32)
    total = array(rows, size, dtype=F32)
    bias = array(blocks, 16, lanes, dtype=F32)
    grads_t = array(blocks, size, lanes)
    own_shape, prev_shape = array(n_own * BLK, lanes), array(n_prev * BLK, lanes)
    ds_shape = array(blocks, count * BLK, lanes)
    far_shape = array(count, rows, size)
    full = array(*queries.shape)
    whole = pltpu.VMEM(queries.shape, BF16)

    causal = call(causal_mask, n_own, 8, [array(BLK, lanes, dtype=F32)], ())[0]
    bias, stat_own, acc_own, p_own, grad_t = call(
        local_forward, n_own, 2,
        [bias, stat, acc, own_shape, grads_t],
        (link_mask, causal, queries, out_grad, key_rows, value_rows),
        places=[smem] + [vmem] * 5,
    )
    stat_near, acc_near, p_prev = call(
        prev_forward, n_prev, 2,
        [stat, acc, prev_shape],
        (queries, k_prev, v_prev, grad_t, bias, stat_own, acc_own),
    )
    dv_far, low_far, fin = call(
        far_scores, n_far, 2,
        [far_shape, ds_shape, stat],
        (queries, grad_t, k_far, bias, stat_near, acc_near),
    )
    dk_far, ds_far, fin = call(
        far_keys, n_far, 2,
        [far_shape, ds_shape, stat],
        (queries, grad_t, v_far, low_far, fin),
    )
    dv_prev, scaled = call(prev_values, n_prev, 1, [total, grads_t], (grad_t, fin, p_prev))
    dk_prev, ds_prev = call(prev_keys, n_prev, 2, [total, prev_shape], (queries, v_prev, fin, p_prev, scaled))
    dk_own, dv_own, output, query_grad = call(
        local_backward, n_own, 5,
        [total, total, full, full],
        (queries, grad_t, keys, values, k_prev, k_far, v_far, fin, acc_near, low_far, p_own, ds_prev, ds_far),
        scratch=[
            pltpu.VMEM(grads_t.shape, BF16), pltpu.VMEM(own_shape.shape, BF16), whole, whole, pltpu.SemaphoreType.DMA((2 * blocks,))
        ],
        lasts=(hbm, hbm),
    )

    def send_back(pending, prev, own):
        levels = [(1, prev)] + [(hop, pending[n].astype(F32)) for n, hop in enumerate(plan.hops)]
        arrived = None
        for n in reversed(range(len(levels))):
            hop, mine = levels[n]
            below = levels[n - 1][0] if n > 0 else 0
            running = mine if arrived is None else mine + arrived.astype(F32)
            arrived = shift(running.astype(BF16), "ctx", below - hop, hop)
        return (own + arrived.astype(F32)).astype(BF16)[None]

    value_grad = send_back(dv_far, dv_prev, dv_own)
    key_grad = send_back(dk_far, dk_prev, dk_own)
    return output, query_grad, key_grad, value_grad


def solution(mesh):
    split = P(("groups", "head"), "ctx", None)

    return jax.shard_map(
        local,
        mesh=mesh,
        in_specs=(split, split, split, split, P(("groups", "ctx"), None)),
        out_specs=(split, split, split, split),
        check_vma=False,
    )
```

profile of v0, /device:TPU:18, one launch (start us, length us, event | category | flops | bytes accessed | tf_op | source)
XLA Modules:
  0.0 42.1 jit_solution(13251321199517527839)
XLA Ops:
  0.6 3.5 %collective-permute-start = (bf16[512,128]{1,0:T(8,128)(2,1)}, bf16[512,128]{1,0:T(8,128)(2,1)S(1)}, u32[]{:S(2)}, u32[]{:S(2)}) collective-permute-start(bf16[512,128]{1,0:T(8,128)(2,1)} %bitcast.10), channel_id=1, source_target_pairs={{0,4},{4,8},{8,12},{1,5},{5,9},{9,13},{2,6},{6,10},{10,14},{3,7},{... | collective-permute-start | bytes 393224 | tf_op jit(solution)/shard_map/ppermute | solution.py:25
  4.1 0.0 copy-start
  4.1 0.0 copy-start.1
  4.1 0.0 copy-start.2
  4.2 0.0 copy-start.3
  4.2 0.0 copy-start.4
  4.2 2.1 %collective-permute-start.2 = (bf16[512,128]{1,0:T(8,128)(2,1)}, bf16[512,128]{1,0:T(8,128)(2,1)S(1)}, u32[]{:S(2)}, u32[]{:S(2)}) collective-permute-start(bf16[512,128]{1,0:T(8,128)(2,1)} %bitcast.12), channel_id=1, source_target_pairs={{0,4},{4,8},{8,12},{1,5},{5,9},{9,13},{2,6},{6,10},{10,14},{3,7},{... | collective-permute-start | bytes 393224 | tf_op jit(solution)/shard_map/ppermute | solution.py:25
  6.2 1.7 %collective-permute-done.k_ref.kp_ref = bf16[512,128]{1,0:T(8,128)(2,1)S(1)} collective-permute-done((bf16[512,128]{1,0:T(8,128)(2,1)}, bf16[512,128]{1,0:T(8,128)(2,1)S(1)}, u32[]{:S(2)}, u32[]{:S(2)}) %collective-permute-start) | collective-permute-done | bytes 131104 | tf_op jit(solution)/shard_map/ppermute | solution.py:25
  8.0 4.2 %collective-permute-start.1 = (bf16[512,128]{1,0:T(8,128)(2,1)S(1)}, bf16[512,128]{1,0:T(8,128)(2,1)S(1)}, u32[]{:S(2)}, u32[]{:S(2)}) collective-permute-start(bf16[512,128]{1,0:T(8,128)(2,1)S(1)} %collective-permute-done.k_ref.kp_ref), channel_id=1, source_target_pairs={{4,8},{8,12},{5,9},{9,13},{6,10},{10,14},{7,11},{11,15},{20,24},{2... | collective-permute-start | bytes 393224 | tf_op jit(solution)/shard_map/ppermute | solution.py:25
  12.2 0.0 collective-permute-done.2.v_ref
  12.2 2.1 %collective-permute-start.3 = (bf16[512,128]{1,0:T(8,128)(2,1)S(1)}, bf16[512,128]{1,0:T(8,128)(2,1)S(1)}, u32[]{:S(2)}, u32[]{:S(2)}) collective-permute-start(bf16[512,128]{1,0:T(8,128)(2,1)S(1)} %collective-permute-done.2.v_ref), channel_id=1, source_target_pairs={{4,8},{8,12},{5,9},{9,13},{6,10},{10,14},{7,11},{11,15},{20,24},{2... | collective-permute-start | bytes 393224 | tf_op jit(solution)/shard_map/ppermute | solution.py:25
  14.3 0.0 copy-done
  14.3 0.0 copy-done.1
  14.3 0.0 copy-done.2
  14.3 0.0 copy-done.3
  14.4 0.0 copy-done.4
  14.4 2.3 %shard_map.85 = (f32[4,16,1024]{2,1,0:T(8,128)S(1)}, f32[4,8,1024]{2,1,0:T(8,128)S(1)}, f32[4,136,1024]{2,1,0:T(8,128)S(1)}, bf16[1152,1024]{1,0:T(8,128)(2,1)S(1)}, bf16[4,128,1024]{2,1,0:T(8,128)(2,1)S(1)}) custom-call(s32[4,11]{1,0:T(4,128)S(1)} %copy-done.4, f32[128,1024]{1,0:T(8,128)S(1)} %shard_map.84.causal_ref, bf16[8,512,128]{2,1,0:T(8,128)(2,1)S(1)} %copy-done, ...), custom_call_target="tpu_custom_call" | custom-call | flops 603979776 | bytes 2097152 | tf_op jit(solution)/shard_map/pallas_call | solution.py:364
  16.6 1.7 %shard_map.86 = (f32[4,8,1024]{2,1,0:T(8,128)S(1)}, f32[4,136,1024]{2,1,0:T(8,128)S(1)}, bf16[896,1024]{1,0:T(8,128)(2,1)S(1)}) custom-call(bf16[8,512,128]{2,1,0:T(8,128)(2,1)S(1)} %copy-done, bf16[512,128]{1,0:T(8,128)(2,1)S(1)} %collective-permute-done.k_ref.kp_ref, bf16[512,128]{1,0:T(8,128)(2,1)S(1)} %collective-permute-done.2.v_ref, ...), custom_call_target="tpu_custom_call" | custom-call | flops 469762048 | bytes 2097152 | tf_op jit(solution)/shard_map/pallas_call | solution.py:364
  18.3 0.0 collective-permute-done.1
  18.3 1.2 %shard_map.87 = (bf16[1,512,128]{2,1,0:T(8,128)(2,1)S(1)}, bf16[4,128,1024]{2,1,0:T(8,128)(2,1)S(1)}, f32[4,8,1024]{2,1,0:T(8,128)S(1)}) custom-call(bf16[8,512,128]{2,1,0:T(8,128)(2,1)S(1)} %copy-done, bf16[4,128,1024]{2,1,0:T(8,128)(2,1)S(1)} %get-tuple-element.26.dot_ref, bf16[1,512,128]{2,1,0:T(8,128)(2,1)S(1)} %bitcast.14, ...), custom_call_target="tpu_custom_call" | custom-call | flops 268435456 | bytes 2097152 | tf_op jit(solution)/shard_map/pallas_call | solution.py:364
  19.6 3.8 %collective-permute-start.6 = (bf16[512,128]{1,0:T(8,128)(2,1)S(1)}, bf16[512,128]{1,0:T(8,128)(2,1)S(1)}, u32[]{:S(2)}, u32[]{:S(2)}) collective-permute-start(bf16[512,128]{1,0:T(8,128)(2,1)S(1)} %bitcast.18), channel_id=1, source_target_pairs={{8,4},{12,8},{9,5},{13,9},{10,6},{14,10},{11,7},{15,11},{24,20},{2... | collective-permute-start | bytes 393224 | tf_op jit(solution)/shard_map/ppermute | solution.py:25
  23.3 0.0 collective-permute-done.3
  23.3 1.0 %shard_map.88 = (bf16[1,512,128]{2,1,0:T(8,128)(2,1)S(1)}, bf16[4,128,1024]{2,1,0:T(8,128)(2,1)S(1)}, f32[4,8,1024]{2,1,0:T(8,128)S(1)}) custom-call(bf16[8,512,128]{2,1,0:T(8,128)(2,1)S(1)} %copy-done, bf16[4,128,1024]{2,1,0:T(8,128)(2,1)S(1)} %get-tuple-element.26.dot_ref, bf16[1,512,128]{2,1,0:T(8,128)(2,1)S(1)} %bitcast.16, ...), custom_call_target="tpu_custom_call" | custom-call | flops 268435456 | bytes 2097152 | tf_op jit(solution)/shard_map/pallas_call | solution.py:364
  24.3 1.9 %collective-permute-start.4 = (bf16[512,128]{1,0:T(8,128)(2,1)S(1)}, bf16[512,128]{1,0:T(8,128)(2,1)S(1)}, u32[]{:S(2)}, u32[]{:S(2)}) collective-permute-start(bf16[512,128]{1,0:T(8,128)(2,1)S(1)} %bitcast.19), channel_id=1, source_target_pairs={{8,4},{12,8},{9,5},{13,9},{10,6},{14,10},{11,7},{15,11},{24,20},{2... | collective-permute-start | bytes 393224 | tf_op jit(solution)/shard_map/ppermute | solution.py:25
  26.2 0.7 %shard_map.89 = (f32[512,128]{1,0:T(8,128)S(1)}, bf16[4,128,1024]{2,1,0:T(8,128)(2,1)S(1)}) custom-call(bf16[4,128,1024]{2,1,0:T(8,128)(2,1)S(1)} %get-tuple-element.26.dot_ref, f32[4,8,1024]{2,1,0:T(8,128)S(1)} %get-tuple-element.34.fin_ref, bf16[896,1024]{1,0:T(8,128)(2,1)S(1)} %get-tuple-element.36.p_ref), custom_call_target="tpu_custom_call" | custom-call | flops 234881024 | bytes 2097152 | tf_op jit(solution)/shard_map/pallas_call | solution.py:364
  26.9 1.3 %shard_map.90 = (f32[512,128]{1,0:T(8,128)S(1)}, bf16[896,1024]{1,0:T(8,128)(2,1)S(1)}) custom-call(bf16[8,512,128]{2,1,0:T(8,128)(2,1)S(1)} %copy-done, bf16[512,128]{1,0:T(8,128)(2,1)S(1)} %collective-permute-done.2.v_ref, f32[4,8,1024]{2,1,0:T(8,128)S(1)} %get-tuple-element.34.fin_ref, bf16[896,1024]{1,0:T(8,128)(2,1)S(1)} %get-tuple-element.36.p_ref, ...), custom_call_target="tpu_custom_call" | custom-call | flops 469762048 | bytes 2097152 | tf_op jit(solution)/shard_map/pallas_call | solution.py:364
  28.2 4.3 %shard_map.91 = (f32[512,128]{1,0:T(8,128)S(1)}, f32[512,128]{1,0:T(8,128)S(1)}, bf16[8,512,128]{2,1,0:T(8,128)(2,1)}, bf16[8,512,128]{2,1,0:T(8,128)(2,1)}) custom-call(bf16[8,512,128]{2,1,0:T(8,128)(2,1)S(1)} %copy-done, bf16[4,128,1024]{2,1,0:T(8,128)(2,1)S(1)} %get-tuple-element.26.dot_ref, bf16[512,128]{1,0:T(8,128)(2,1)S(1)} %bitcast.11, ...), custom_call_target="tpu_custom_call" | custom-call | flops 1509949440 | bytes 2097152 | tf_op jit(solution)/shard_map/pallas_call | solution.py:364
  32.5 0.0 collective-permute-done.6
  32.6 1.9 %collective-permute-start.7 = (bf16[512,128]{1,0:T(8,128)(2,1)S(1)}, bf16[512,128]{1,0:T(8,128)(2,1)S(1)}, u32[]{:S(2)}, u32[]{:S(2)}) collective-permute-start(bf16[512,128]{1,0:T(8,128)(2,1)S(1)} %add_convert_fusion.1), channel_id=1, source_target_pairs={{4,0},{8,4},{12,8},{5,1},{9,5},{13,9},{6,2},{10,6},{14,10},{7,3},{... | collective-permute-start | bytes 393224 | tf_op jit(solution)/shard_map/ppermute | solution.py:25
  34.5 0.0 collective-permute-done.4
  34.5 1.9 %collective-permute-start.5 = (bf16[512,128]{1,0:T(8,128)(2,1)S(1)}, bf16[512,128]{1,0:T(8,128)(2,1)S(1)}, u32[]{:S(2)}, u32[]{:S(2)}) collective-permute-start(bf16[512,128]{1,0:T(8,128)(2,1)S(1)} %add_convert_fusion.3), channel_id=1, source_target_pairs={{4,0},{8,4},{12,8},{5,1},{9,5},{13,9},{6,2},{10,6},{14,10},{7,3},{... | collective-permute-start | bytes 393224 | tf_op jit(solution)/shard_map/ppermute | solution.py:25
  36.5 3.0 %collective-permute-done.7 = bf16[512,128]{1,0:T(8,128)(2,1)S(1)} collective-permute-done((bf16[512,128]{1,0:T(8,128)(2,1)S(1)}, bf16[512,128]{1,0:T(8,128)(2,1)S(1)}, u32[]{:S(2)}, u32[]{:S(2)}) %collective-permute-start.7) | collective-permute-done | bytes 131104 | tf_op jit(solution)/shard_map/ppermute | solution.py:25
  39.4 0.7 %fusion.1 = bf16[1,512,128]{2,1,0:T(8,128)(2,1)} fusion(f32[512,128]{1,0:T(8,128)S(1)} %get-tuple-element.45, bf16[512,128]{1,0:T(8,128)(2,1)S(1)} %collective-permute-done.7), kind=kLoop, calls=%fused_computation.5 | loop fusion | flops 196608 | bytes 524288 | tf_op jit(solution)/shard_map/broadcast_in_dim | solution.py:431
  40.1 1.3 %collective-permute-done.5 = bf16[512,128]{1,0:T(8,128)(2,1)S(1)} collective-permute-done((bf16[512,128]{1,0:T(8,128)(2,1)S(1)}, bf16[512,128]{1,0:T(8,128)(2,1)S(1)}, u32[]{:S(2)}, u32[]{:S(2)}) %collective-permute-start.5) | collective-permute-done | bytes 131104 | tf_op jit(solution)/shard_map/ppermute | solution.py:25
  41.4 0.7 %fusion = bf16[1,512,128]{2,1,0:T(8,128)(2,1)} fusion(f32[512,128]{1,0:T(8,128)S(1)} %get-tuple-element.42, bf16[512,128]{1,0:T(8,128)(2,1)S(1)} %collective-permute-done.5), kind=kLoop, calls=%fused_computation.4 | loop fusion | flops 196608 | bytes 524288 | tf_op jit(solution)/shard_map/broadcast_in_dim | solution.py:431
  (3 shorter events, 0.1 us)
Async XLA Ops:
  0.6 7.3 %collective-permute-start = (bf16[512,128]{1,0:T(8,128)(2,1)}, bf16[512,128]{1,0:T(8,128)(2,1)S(1)}, u32[]{:S(2)}, u32[]{:S(2)}) collective-permute-start(bf16[512,128]{1,0:T(8,128)(2,1)} %bitcast.10), channel_id=1, source_target_pairs={{0,4},{4,8},{8,12},{1,5},{5,9},{9,13},{2,6},{6,10},{10,14},{3,7},{... | collective-permute-start | bytes 393224 | tf_op jit(solution)/shard_map/ppermute | solution.py:25
  4.1 10.2 %copy-start = (bf16[8,512,128]{2,1,0:T(8,128)(2,1)S(1)}, bf16[8,512,128]{2,1,0:T(8,128)(2,1)}, u32[]{:S(2)}) copy-start(bf16[8,512,128]{2,1,0:T(8,128)(2,1)} %q_ref.11) | copy-start | bytes 3145732
  4.1 10.2 %copy-start.1 = (bf16[8,512,128]{2,1,0:T(8,128)(2,1)S(1)}, bf16[8,512,128]{2,1,0:T(8,128)(2,1)}, u32[]{:S(2)}) copy-start(bf16[8,512,128]{2,1,0:T(8,128)(2,1)} %do_ref.1) | copy-start | bytes 3145732
  4.1 10.2 %copy-start.2 = (bf16[1,512,128]{2,1,0:T(8,128)(2,1)S(1)}, bf16[1,512,128]{2,1,0:T(8,128)(2,1)}, u32[]{:S(2)}) copy-start(bf16[1,512,128]{2,1,0:T(8,128)(2,1)} %k_ref.1) | copy-start | bytes 393220
  4.2 10.2 %copy-start.3 = (bf16[1,512,128]{2,1,0:T(8,128)(2,1)S(1)}, bf16[1,512,128]{2,1,0:T(8,128)(2,1)}, u32[]{:S(2)}) copy-start(bf16[1,512,128]{2,1,0:T(8,128)(2,1)} %v_ref.1) | copy-start | bytes 393220
  4.2 10.2 %copy-start.4 = (s32[4,11]{1,0:T(4,128)S(1)}, s32[4,11]{1,0:T(4,128)}, u32[]{:S(2)}) copy-start(s32[4,11]{1,0:T(4,128)} %link_ref.1) | copy-start | bytes 532
  4.2 8.0 %collective-permute-start.2 = (bf16[512,128]{1,0:T(8,128)(2,1)}, bf16[512,128]{1,0:T(8,128)(2,1)S(1)}, u32[]{:S(2)}, u32[]{:S(2)}) collective-permute-start(bf16[512,128]{1,0:T(8,128)(2,1)} %bitcast.12), channel_id=1, source_target_pairs={{0,4},{4,8},{8,12},{1,5},{5,9},{9,13},{2,6},{6,10},{10,14},{3,7},{... | collective-permute-start | bytes 393224 | tf_op jit(solution)/shard_map/ppermute | solution.py:25
  8.0 10.3 %collective-permute-start.1 = (bf16[512,128]{1,0:T(8,128)(2,1)S(1)}, bf16[512,128]{1,0:T(8,128)(2,1)S(1)}, u32[]{:S(2)}, u32[]{:S(2)}) collective-permute-start(bf16[512,128]{1,0:T(8,128)(2,1)S(1)} %collective-permute-done.k_ref.kp_ref), channel_id=1, source_target_pairs={{4,8},{8,12},{5,9},{9,13},{6,10},{10,14},{7,11},{11,15},{20,24},{2... | collective-permute-start | bytes 393224 | tf_op jit(solution)/shard_map/ppermute | solution.py:25
  12.2 11.2 %collective-permute-start.3 = (bf16[512,128]{1,0:T(8,128)(2,1)S(1)}, bf16[512,128]{1,0:T(8,128)(2,1)S(1)}, u32[]{:S(2)}, u32[]{:S(2)}) collective-permute-start(bf16[512,128]{1,0:T(8,128)(2,1)S(1)} %collective-permute-done.2.v_ref), channel_id=1, source_target_pairs={{4,8},{8,12},{5,9},{9,13},{6,10},{10,14},{7,11},{11,15},{20,24},{2... | collective-permute-start | bytes 393224 | tf_op jit(solution)/shard_map/ppermute | solution.py:25
  19.6 13.0 %collective-permute-start.6 = (bf16[512,128]{1,0:T(8,128)(2,1)S(1)}, bf16[512,128]{1,0:T(8,128)(2,1)S(1)}, u32[]{:S(2)}, u32[]{:S(2)}) collective-permute-start(bf16[512,128]{1,0:T(8,128)(2,1)S(1)} %bitcast.18), channel_id=1, source_target_pairs={{8,4},{12,8},{9,5},{13,9},{10,6},{14,10},{11,7},{15,11},{24,20},{2... | collective-permute-start | bytes 393224 | tf_op jit(solution)/shard_map/ppermute | solution.py:25
  24.3 10.2 %collective-permute-start.4 = (bf16[512,128]{1,0:T(8,128)(2,1)S(1)}, bf16[512,128]{1,0:T(8,128)(2,1)S(1)}, u32[]{:S(2)}, u32[]{:S(2)}) collective-permute-start(bf16[512,128]{1,0:T(8,128)(2,1)S(1)} %bitcast.19), channel_id=1, source_target_pairs={{8,4},{12,8},{9,5},{13,9},{10,6},{14,10},{11,7},{15,11},{24,20},{2... | collective-permute-start | bytes 393224 | tf_op jit(solution)/shard_map/ppermute | solution.py:25
  32.6 6.9 %collective-permute-start.7 = (bf16[512,128]{1,0:T(8,128)(2,1)S(1)}, bf16[512,128]{1,0:T(8,128)(2,1)S(1)}, u32[]{:S(2)}, u32[]{:S(2)}) collective-permute-start(bf16[512,128]{1,0:T(8,128)(2,1)S(1)} %add_convert_fusion.1), channel_id=1, source_target_pairs={{4,0},{8,4},{12,8},{5,1},{9,5},{13,9},{6,2},{10,6},{14,10},{7,3},{... | collective-permute-start | bytes 393224 | tf_op jit(solution)/shard_map/ppermute | solution.py:25
  34.5 6.9 %collective-permute-start.5 = (bf16[512,128]{1,0:T(8,128)(2,1)S(1)}, bf16[512,128]{1,0:T(8,128)(2,1)S(1)}, u32[]{:S(2)}, u32[]{:S(2)}) collective-permute-start(bf16[512,128]{1,0:T(8,128)(2,1)S(1)} %add_convert_fusion.3), channel_id=1, source_target_pairs={{4,0},{8,4},{12,8},{5,1},{9,5},{13,9},{6,2},{10,6},{14,10},{7,3},{... | collective-permute-start | bytes 393224 | tf_op jit(solution)/shard_map/ppermute | solution.py:25
where the time goes:
time: 42.4 us; the launch traced here: 42.1 us
  starting transfers between devices  21.3 us (50%)
  Pallas kernels  12.4 us (29%)
  waiting for transfers between devices  6 us (14%)
  other arithmetic  1.43 us (3%)
  between operations  0.88 us (2%)
    ppermute x8, starting transfers between devices, shift(): lax.ppermute(value, axis, [(n, n + steps) for n in range(holders, count)...  21.3 us
    pallas_call x8, Pallas kernels, call(): pl.pallas_call(functools.partial(body, plan), in_specs=places or [vmem] *...  12.4 us
    ppermute x8, waiting for transfers between devices, shift(): lax.ppermute(value, axis, [(n, n + steps) for n in range(holders, count)...  6 us
    broadcast_in_dim x2, other arithmetic, send_back(): return (own + arrived.astype(F32)).astype(BF16)[None]  1.37 us
  transfers between devices with their start and end apart: 8, of which 3 were waited for; matrix products, arithmetic and copies ran while one was open for 2% of the time, Pallas kernels for 30%

commit v1 on v0

--- a/solution.py
+++ b/solution.py
@@ -180,6 +180,10 @@
         stat_ref[i, 2:3, lanes] = jnp.sum(acc[:size] * dot_ref[i, :, lanes].astype(F32), axis=0, keepdims=True)
 
     staged(plan.items(WIDE), first, second)
+
+
+def has_far(plan):
+    return (lax.axis_index("ctx") + 1) * plan.blocks > plan.entries[plan.far[0]][1]
 
 
 def far_scores(plan, q_ref, dot_ref, k_ref, bias_ref, stat_ref, acc_ref, dv_ref, low_ref, fin_ref):
@@ -209,7 +213,19 @@
             for f in range(count):
                 dv_ref[f, block(i)] = dv[block(f)].astype(BF16)
 
-    staged(plan.items(FAR_WIDE), first, second)
+    @pl.when(has_far(plan))
+    def _():
+        staged(plan.items(FAR_WIDE), first, second)
+
+    @pl.when(jnp.logical_not(has_far(plan)))
+    def _():
+        dv_ref[...] = jnp.zeros_like(dv_ref)
+        low_ref[...] = jnp.zeros_like(low_ref)
+        for i in range(plan.blocks):
+            inverse = 1.0 / acc_ref[i, size : size + 1, :]
+            fin_ref[i, 0:1, :] = jnp.exp2(stat_ref[i, 0:1, :] - stat_ref[i, 1:2, :]) * inverse
+            fin_ref[i, 1:2, :] = inverse
+            fin_ref[i, 2:3, :] = stat_ref[i, 2:3, :] * inverse
 
 
 def far_keys(plan, q_ref, dot_ref, v_ref, low_ref, fin_in, dk_ref, ds_ref, fin_ref):
@@ -227,14 +243,22 @@
         products = weights * grad_w
         row_dot = fin_in[i, 2:3, lanes] + jnp.sum(products, axis=0, keepdims=True)
         ds_ref[i, :, lanes] = (products - weights * row_dot).astype(BF16)
-        fin_ref[i, 0:2, lanes] = fin_in[i, 0:2, lanes]
         fin_ref[i, 2:3, lanes] = row_dot
         if lanes.stop == plan.lanes:
             dk = dot_nn(ds_ref[i], rows_of(q_ref, slice(0, plan.heads), i, size)) * plan.inv_root
             for f in range(count):
                 dk_ref[f, block(i)] = dk[block(f)].astype(BF16)
 
-    staged(plan.items(FAR_WIDE), first, second)
+    fin_ref[...] = fin_in[...]
+
+    @pl.when(has_far(plan))
+    def _():
+        staged(plan.items(FAR_WIDE), first, second)
+
+    @pl.when(jnp.logical_not(has_far(plan)))
+    def _():
+        dk_ref[...] = jnp.zeros_like(dk_ref)
+        ds_ref[...] = jnp.zeros_like(ds_ref)
 
 
 def add_blocks(sums, slots, parts):
@@ -329,6 +353,18 @@
         copy.wait()
 
 
+def finish(plan, dk_ref, dv_ref, kg_ref, vg_ref, k_hbm, v_hbm, k_out, v_out, sems):
+    copies = []
+    for n, (own, arrived, out, target) in enumerate(
+        ((dv_ref, vg_ref, v_out, v_hbm), (dk_ref, kg_ref, k_out, k_hbm))
+    ):
+        out[0] = (own[...] + arrived[...].astype(F32)).astype(BF16)
+        copies.append(pltpu.make_async_copy(out, target, sems.at[n]))
+        copies[n].start()
+    for copy in copies:
+        copy.wait()
+
+
 def local(queries, key_rows, value_rows, out_grad, link_mask):
     heads, rows, size = queries.shape
     blocks = rows // BLK
@@ -420,7 +456,7 @@
         lasts=(hbm, hbm),
     )
 
-    def send_back(pending, prev, own):
+    def send_back(pending, prev):
         levels = [(1, prev)] + [(hop, pending[n].astype(F32)) for n, hop in enumerate(plan.hops)]
         arrived = None
         for n in reversed(range(len(levels))):
@@ -428,10 +464,16 @@
             below = levels[n - 1][0] if n > 0 else 0
             running = mine if arrived is None else mine + arrived.astype(F32)
             arrived = shift(running.astype(BF16), "ctx", below - hop, hop)
-        return (own + arrived.astype(F32)).astype(BF16)[None]
-
-    value_grad = send_back(dv_far, dv_prev, dv_own)
-    key_grad = send_back(dk_far, dk_prev, dk_own)
+        return arrived
+
+    v_arrived = send_back(dv_far, dv_prev)
+    k_arrived = send_back(dk_far, dk_prev)
+    line = array(1, rows, size)
+    key_grad, value_grad = call(
+        finish, 1, 1, [line, line], (dk_own, dv_own, k_arrived, v_arrived),
+        scratch=[pltpu.VMEM(line.shape, BF16), pltpu.VMEM(line.shape, BF16), pltpu.SemaphoreType.DMA((2,))],
+        lasts=(hbm, hbm),
+    )
     return output, query_grad, key_grad, value_grad
 
 

time: 42.4 us -> 39 us (0.920)
  the two profiles are of different devices: /device:TPU:18 before, /device:TPU:0 now
where the time goes in v1:
time: 39 us; the launch traced here: 38.7 us
  starting transfers between devices  13.8 us (35%)
  waiting for transfers between devices  12.7 us (33%)
  Pallas kernels  11.2 us (29%)
  between operations  0.88 us (2%)
    ppermute x8, starting transfers between devices, shift(): lax.ppermute(value, axis, [(n, n + steps) for n in range(holders, count)...  13.8 us
    ppermute x8, waiting for transfers between devices, shift(): lax.ppermute(value, axis, [(n, n + steps) for n in range(holders, count)...  12.7 us
    pallas_call x9, Pallas kernels, call(): pl.pallas_call(functools.partial(body, plan), in_specs=places or [vmem] *...  11.2 us
  transfers between devices with their start and end apart: 8, of which 3 were waited for; matrix products, arithmetic and copies ran while one was open for 0% of the time, Pallas kernels for 27%

profile of v1, /device:TPU:0, one launch (start us, length us, event | category | flops | bytes accessed | tf_op | source)
XLA Modules:
  0.0 38.7 jit_solution(18026948128602412353)
XLA Ops:
  0.6 5.0 %collective-permute-start = (bf16[512,128]{1,0:T(8,128)(2,1)}, bf16[512,128]{1,0:T(8,128)(2,1)S(1)}, u32[]{:S(2)}, u32[]{:S(2)}) collective-permute-start(bf16[512,128]{1,0:T(8,128)(2,1)} %bitcast.6), channel_id=1, source_target_pairs={{0,4},{4,8},{8,12},{1,5},{5,9},{9,13},{2,6},{6,10},{10,14},{3,7},{... | collective-permute-start | bytes 393224 | tf_op jit(solution)/shard_map/ppermute | solution.py:25
  5.6 0.0 copy-start
  5.6 0.0 copy-start.1
  5.6 0.0 copy-start.2
  5.6 0.0 copy-start.3
  5.6 0.0 copy-start.4
  5.7 3.6 %collective-permute-start.2 = (bf16[512,128]{1,0:T(8,128)(2,1)}, bf16[512,128]{1,0:T(8,128)(2,1)S(1)}, u32[]{:S(2)}, u32[]{:S(2)}) collective-permute-start(bf16[512,128]{1,0:T(8,128)(2,1)} %bitcast.8), channel_id=1, source_target_pairs={{0,4},{4,8},{8,12},{1,5},{5,9},{9,13},{2,6},{6,10},{10,14},{3,7},{... | collective-permute-start | bytes 393224 | tf_op jit(solution)/shard_map/ppermute | solution.py:25
  9.3 0.0 collective-permute-done.k_ref.kp_ref
  9.3 0.7 %collective-permute-start.1 = (bf16[512,128]{1,0:T(8,128)(2,1)S(1)}, bf16[512,128]{1,0:T(8,128)(2,1)S(1)}, u32[]{:S(2)}, u32[]{:S(2)}) collective-permute-start(bf16[512,128]{1,0:T(8,128)(2,1)S(1)} %collective-permute-done.k_ref.kp_ref), channel_id=1, source_target_pairs={{4,8},{8,12},{5,9},{9,13},{6,10},{10,14},{7,11},{11,15},{20,24},{2... | collective-permute-start | bytes 393224 | tf_op jit(solution)/shard_map/ppermute | solution.py:25
  10.0 2.1 %collective-permute-done.2.v_ref = bf16[512,128]{1,0:T(8,128)(2,1)S(1)} collective-permute-done((bf16[512,128]{1,0:T(8,128)(2,1)}, bf16[512,128]{1,0:T(8,128)(2,1)S(1)}, u32[]{:S(2)}, u32[]{:S(2)}) %collective-permute-start.2) | collective-permute-done | bytes 131104 | tf_op jit(solution)/shard_map/ppermute | solution.py:25
  12.1 0.7 %collective-permute-start.3 = (bf16[512,128]{1,0:T(8,128)(2,1)S(1)}, bf16[512,128]{1,0:T(8,128)(2,1)S(1)}, u32[]{:S(2)}, u32[]{:S(2)}) collective-permute-start(bf16[512,128]{1,0:T(8,128)(2,1)S(1)} %collective-permute-done.2.v_ref), channel_id=1, source_target_pairs={{4,8},{8,12},{5,9},{9,13},{6,10},{10,14},{7,11},{11,15},{20,24},{2... | collective-permute-start | bytes 393224 | tf_op jit(solution)/shard_map/ppermute | solution.py:25
  12.8 0.0 copy-done
  12.8 0.0 copy-done.1
  12.8 0.0 copy-done.2
  12.8 0.0 copy-done.3
  12.8 0.0 copy-done.4
  12.8 2.3 %shard_map.85 = (f32[4,16,1024]{2,1,0:T(8,128)S(1)}, f32[4,8,1024]{2,1,0:T(8,128)S(1)}, f32[4,136,1024]{2,1,0:T(8,128)S(1)}, bf16[1152,1024]{1,0:T(8,128)(2,1)S(1)}, bf16[4,128,1024]{2,1,0:T(8,128)(2,1)S(1)}) custom-call(s32[4,11]{1,0:T(4,128)S(1)} %copy-done.4, f32[128,1024]{1,0:T(8,128)S(1)} %shard_map.84.causal_ref, bf16[8,512,128]{2,1,0:T(8,128)(2,1)S(1)} %copy-done, ...), custom_call_target="tpu_custom_call" | custom-call | flops 603979776 | bytes 2097152 | tf_op jit(solution)/shard_map/pallas_call | solution.py:400
  15.1 1.7 %shard_map.86 = (f32[4,8,1024]{2,1,0:T(8,128)S(1)}, f32[4,136,1024]{2,1,0:T(8,128)S(1)}, bf16[896,1024]{1,0:T(8,128)(2,1)S(1)}) custom-call(bf16[8,512,128]{2,1,0:T(8,128)(2,1)S(1)} %copy-done, bf16[512,128]{1,0:T(8,128)(2,1)S(1)} %collective-permute-done.k_ref.kp_ref, bf16[512,128]{1,0:T(8,128)(2,1)S(1)} %collective-permute-done.2.v_ref, ...), custom_call_target="tpu_custom_call" | custom-call | flops 469762048 | bytes 2097152 | tf_op jit(solution)/shard_map/pallas_call | solution.py:400
  16.8 0.0 collective-permute-done.1
  16.8 0.1 shard_map.87
  16.9 0.7 %collective-permute-start.6 = (bf16[512,128]{1,0:T(8,128)(2,1)S(1)}, bf16[512,128]{1,0:T(8,128)(2,1)S(1)}, u32[]{:S(2)}, u32[]{:S(2)}) collective-permute-start(bf16[512,128]{1,0:T(8,128)(2,1)S(1)} %bitcast.14), channel_id=1, source_target_pairs={{8,4},{12,8},{9,5},{13,9},{10,6},{14,10},{11,7},{15,11},{24,20},{2... | collective-permute-start | bytes 393224 | tf_op jit(solution)/shard_map/ppermute | solution.py:25
  17.6 0.0 collective-permute-done.3
  17.6 0.1 shard_map.88
  17.7 0.7 %collective-permute-start.4 = (bf16[512,128]{1,0:T(8,128)(2,1)S(1)}, bf16[512,128]{1,0:T(8,128)(2,1)S(1)}, u32[]{:S(2)}, u32[]{:S(2)}) collective-permute-start(bf16[512,128]{1,0:T(8,128)(2,1)S(1)} %bitcast.15), channel_id=1, source_target_pairs={{8,4},{12,8},{9,5},{13,9},{10,6},{14,10},{11,7},{15,11},{24,20},{2... | collective-permute-start | bytes 393224 | tf_op jit(solution)/shard_map/ppermute | solution.py:25
  18.4 0.7 %shard_map.89 = (f32[512,128]{1,0:T(8,128)S(1)}, bf16[4,128,1024]{2,1,0:T(8,128)(2,1)S(1)}) custom-call(bf16[4,128,1024]{2,1,0:T(8,128)(2,1)S(1)} %get-tuple-element.28.dot_ref, f32[4,8,1024]{2,1,0:T(8,128)S(1)} %get-tuple-element.36.fin_ref, bf16[896,1024]{1,0:T(8,128)(2,1)S(1)} %get-tuple-element.38.p_ref), custom_call_target="tpu_custom_call" | custom-call | flops 234881024 | bytes 2097152 | tf_op jit(solution)/shard_map/pallas_call | solution.py:400
  19.0 1.3 %shard_map.90 = (f32[512,128]{1,0:T(8,128)S(1)}, bf16[896,1024]{1,0:T(8,128)(2,1)S(1)}) custom-call(bf16[8,512,128]{2,1,0:T(8,128)(2,1)S(1)} %copy-done, bf16[512,128]{1,0:T(8,128)(2,1)S(1)} %collective-permute-done.2.v_ref, f32[4,8,1024]{2,1,0:T(8,128)S(1)} %get-tuple-element.36.fin_ref, bf16[896,1024]{1,0:T(8,128)(2,1)S(1)} %get-tuple-element.38.p_ref, ...), custom_call_target="tpu_custom_call" | custom-call | flops 469762048 | bytes 2097152 | tf_op jit(solution)/shard_map/pallas_call | solution.py:400
  20.3 0.0 collective-permute-done.6
  20.3 1.3 %collective-permute-start.7 = (bf16[512,128]{1,0:T(8,128)(2,1)S(1)}, bf16[512,128]{1,0:T(8,128)(2,1)S(1)}, u32[]{:S(2)}, u32[]{:S(2)}) collective-permute-start(bf16[512,128]{1,0:T(8,128)(2,1)S(1)} %add_convert_fusion), channel_id=1, source_target_pairs={{4,0},{8,4},{12,8},{5,1},{9,5},{13,9},{6,2},{10,6},{14,10},{7,3},{... | collective-permute-start | bytes 393224 | tf_op jit(solution)/shard_map/ppermute | solution.py:25
  21.6 0.0 collective-permute-done.4
  21.7 1.3 %collective-permute-start.5 = (bf16[512,128]{1,0:T(8,128)(2,1)S(1)}, bf16[512,128]{1,0:T(8,128)(2,1)S(1)}, u32[]{:S(2)}, u32[]{:S(2)}) collective-permute-start(bf16[512,128]{1,0:T(8,128)(2,1)S(1)} %add_convert_fusion.1), channel_id=1, source_target_pairs={{4,0},{8,4},{12,8},{5,1},{9,5},{13,9},{6,2},{10,6},{14,10},{7,3},{... | collective-permute-start | bytes 393224 | tf_op jit(solution)/shard_map/ppermute | solution.py:25
  23.0 4.3 %shard_map.91 = (f32[512,128]{1,0:T(8,128)S(1)}, f32[512,128]{1,0:T(8,128)S(1)}, bf16[8,512,128]{2,1,0:T(8,128)(2,1)}, bf16[8,512,128]{2,1,0:T(8,128)(2,1)}) custom-call(bf16[8,512,128]{2,1,0:T(8,128)(2,1)S(1)} %copy-done, bf16[4,128,1024]{2,1,0:T(8,128)(2,1)S(1)} %get-tuple-element.28.dot_ref, bf16[512,128]{1,0:T(8,128)(2,1)S(1)} %bitcast.7, ...), custom_call_target="tpu_custom_call" | custom-call | flops 1509949440 | bytes 2097152 | tf_op jit(solution)/shard_map/pallas_call | solution.py:400
  27.3 9.3 %collective-permute-done.7.vg_ref = bf16[512,128]{1,0:T(8,128)(2,1)S(1)} collective-permute-done((bf16[512,128]{1,0:T(8,128)(2,1)S(1)}, bf16[512,128]{1,0:T(8,128)(2,1)S(1)}, u32[]{:S(2)}, u32[]{:S(2)}) %collective-permute-start.7) | collective-permute-done | bytes 131104 | tf_op jit(solution)/shard_map/ppermute | solution.py:25
  36.6 1.4 %collective-permute-done.5.kg_ref = bf16[512,128]{1,0:T(8,128)(2,1)S(1)} collective-permute-done((bf16[512,128]{1,0:T(8,128)(2,1)S(1)}, bf16[512,128]{1,0:T(8,128)(2,1)S(1)}, u32[]{:S(2)}, u32[]{:S(2)}) %collective-permute-start.5) | collective-permute-done | bytes 131104 | tf_op jit(solution)/shard_map/ppermute | solution.py:25
  38.0 0.7 %shard_map.92 = (bf16[1,512,128]{2,1,0:T(8,128)(2,1)}, bf16[1,512,128]{2,1,0:T(8,128)(2,1)}) custom-call(f32[512,128]{1,0:T(8,128)S(1)} %get-tuple-element.44.dk_ref, f32[512,128]{1,0:T(8,128)S(1)} %get-tuple-element.45.dv_ref, bf16[512,128]{1,0:T(8,128)(2,1)S(1)} %collective-permute-done.5.kg_ref, bf16[512,128]{1,0:T(8,128)(2,1)S(1)} %collective-permute-done.7.vg_ref), custom_call_target="tpu_custom_call" | custom-call | flops 33554432 | bytes 2097152 | tf_op jit(solution)/shard_map/pallas_call | solution.py:400
  (3 shorter events, 0.1 us)
Async XLA Ops:
  0.6 8.6 %collective-permute-start = (bf16[512,128]{1,0:T(8,128)(2,1)}, bf16[512,128]{1,0:T(8,128)(2,1)S(1)}, u32[]{:S(2)}, u32[]{:S(2)}) collective-permute-start(bf16[512,128]{1,0:T(8,128)(2,1)} %bitcast.6), channel_id=1, source_target_pairs={{0,4},{4,8},{8,12},{1,5},{5,9},{9,13},{2,6},{6,10},{10,14},{3,7},{... | collective-permute-start | bytes 393224 | tf_op jit(solution)/shard_map/ppermute | solution.py:25
  5.6 7.2 %copy-start = (bf16[8,512,128]{2,1,0:T(8,128)(2,1)S(1)}, bf16[8,512,128]{2,1,0:T(8,128)(2,1)}, u32[]{:S(2)}) copy-start(bf16[8,512,128]{2,1,0:T(8,128)(2,1)} %q_ref.11) | copy-start | bytes 3145732
  5.6 7.2 %copy-start.1 = (bf16[8,512,128]{2,1,0:T(8,128)(2,1)S(1)}, bf16[8,512,128]{2,1,0:T(8,128)(2,1)}, u32[]{:S(2)}) copy-start(bf16[8,512,128]{2,1,0:T(8,128)(2,1)} %do_ref.1) | copy-start | bytes 3145732
  5.6 7.2 %copy-start.2 = (bf16[1,512,128]{2,1,0:T(8,128)(2,1)S(1)}, bf16[1,512,128]{2,1,0:T(8,128)(2,1)}, u32[]{:S(2)}) copy-start(bf16[1,512,128]{2,1,0:T(8,128)(2,1)} %k_ref.1) | copy-start | bytes 393220
  5.6 7.2 %copy-start.3 = (bf16[1,512,128]{2,1,0:T(8,128)(2,1)S(1)}, bf16[1,512,128]{2,1,0:T(8,128)(2,1)}, u32[]{:S(2)}) copy-start(bf16[1,512,128]{2,1,0:T(8,128)(2,1)} %v_ref.1) | copy-start | bytes 393220
  5.6 7.2 %copy-start.4 = (s32[4,11]{1,0:T(4,128)S(1)}, s32[4,11]{1,0:T(4,128)}, u32[]{:S(2)}) copy-start(s32[4,11]{1,0:T(4,128)} %link_ref.1) | copy-start | bytes 532
  5.7 6.4 %collective-permute-start.2 = (bf16[512,128]{1,0:T(8,128)(2,1)}, bf16[512,128]{1,0:T(8,128)(2,1)S(1)}, u32[]{:S(2)}, u32[]{:S(2)}) collective-permute-start(bf16[512,128]{1,0:T(8,128)(2,1)} %bitcast.8), channel_id=1, source_target_pairs={{0,4},{4,8},{8,12},{1,5},{5,9},{9,13},{2,6},{6,10},{10,14},{3,7},{... | collective-permute-start | bytes 393224 | tf_op jit(solution)/shard_map/ppermute | solution.py:25
  9.3 7.5 %collective-permute-start.1 = (bf16[512,128]{1,0:T(8,128)(2,1)S(1)}, bf16[512,128]{1,0:T(8,128)(2,1)S(1)}, u32[]{:S(2)}, u32[]{:S(2)}) collective-permute-start(bf16[512,128]{1,0:T(8,128)(2,1)S(1)} %collective-permute-done.k_ref.kp_ref), channel_id=1, source_target_pairs={{4,8},{8,12},{5,9},{9,13},{6,10},{10,14},{7,11},{11,15},{20,24},{2... | collective-permute-start | bytes 393224 | tf_op jit(solution)/shard_map/ppermute | solution.py:25
  12.1 5.5 %collective-permute-start.3 = (bf16[512,128]{1,0:T(8,128)(2,1)S(1)}, bf16[512,128]{1,0:T(8,128)(2,1)S(1)}, u32[]{:S(2)}, u32[]{:S(2)}) collective-permute-start(bf16[512,128]{1,0:T(8,128)(2,1)S(1)} %collective-permute-done.2.v_ref), channel_id=1, source_target_pairs={{4,8},{8,12},{5,9},{9,13},{6,10},{10,14},{7,11},{11,15},{20,24},{2... | collective-permute-start | bytes 393224 | tf_op jit(solution)/shard_map/ppermute | solution.py:25
  16.9 3.4 %collective-permute-start.6 = (bf16[512,128]{1,0:T(8,128)(2,1)S(1)}, bf16[512,128]{1,0:T(8,128)(2,1)S(1)}, u32[]{:S(2)}, u32[]{:S(2)}) collective-permute-start(bf16[512,128]{1,0:T(8,128)(2,1)S(1)} %bitcast.14), channel_id=1, source_target_pairs={{8,4},{12,8},{9,5},{13,9},{10,6},{14,10},{11,7},{15,11},{24,20},{2... | collective-permute-start | bytes 393224 | tf_op jit(solution)/shard_map/ppermute | solution.py:25
  17.7 4.0 %collective-permute-start.4 = (bf16[512,128]{1,0:T(8,128)(2,1)S(1)}, bf16[512,128]{1,0:T(8,128)(2,1)S(1)}, u32[]{:S(2)}, u32[]{:S(2)}) collective-permute-start(bf16[512,128]{1,0:T(8,128)(2,1)S(1)} %bitcast.15), channel_id=1, source_target_pairs={{8,4},{12,8},{9,5},{13,9},{10,6},{14,10},{11,7},{15,11},{24,20},{2... | collective-permute-start | bytes 393224 | tf_op jit(solution)/shard_map/ppermute | solution.py:25
  20.3 16.2 %collective-permute-start.7 = (bf16[512,128]{1,0:T(8,128)(2,1)S(1)}, bf16[512,128]{1,0:T(8,128)(2,1)S(1)}, u32[]{:S(2)}, u32[]{:S(2)}) collective-permute-start(bf16[512,128]{1,0:T(8,128)(2,1)S(1)} %add_convert_fusion), channel_id=1, source_target_pairs={{4,0},{8,4},{12,8},{5,1},{9,5},{13,9},{6,2},{10,6},{14,10},{7,3},{... | collective-permute-start | bytes 393224 | tf_op jit(solution)/shard_map/ppermute | solution.py:25
  21.7 16.3 %collective-permute-start.5 = (bf16[512,128]{1,0:T(8,128)(2,1)S(1)}, bf16[512,128]{1,0:T(8,128)(2,1)S(1)}, u32[]{:S(2)}, u32[]{:S(2)}) collective-permute-start(bf16[512,128]{1,0:T(8,128)(2,1)S(1)} %add_convert_fusion.1), channel_id=1, source_target_pairs={{4,0},{8,4},{12,8},{5,1},{9,5},{13,9},{6,2},{10,6},{14,10},{7,3},{... | collective-permute-start | bytes 393224 | tf_op jit(solution)/shard_map/ppermute | solution.py:25

commit v2 on v1

--- a/solution.py
+++ b/solution.py
@@ -23,6 +23,20 @@
 def shift(value, axis, steps, holders):
     count = lax.axis_size(axis)
     return lax.ppermute(value, axis, [(n, n + steps) for n in range(holders, count) if 0 <= n + steps < count])
+
+
+def two_up(own, near, axis):
+    count = lax.axis_size(axis)
+    straight = lax.ppermute(own, axis, [(n, n + 2) for n in range(0, count - 2, 2)])
+    relayed = lax.ppermute(near, axis, [(n, n + 1) for n in range(2, count - 1, 2)])
+    return straight + relayed
+
+
+def far_rows(own, near, hops):
+    rows = [two_up(own, near, "ctx")]
+    for at, hop in zip(hops, hops[1:]):
+        rows.append(shift(rows[-1], "ctx", hop - at, at))
+    return rows[0][None] if len(rows) == 1 else jnp.stack(rows)
 
 
 def slot_table(block_count, ctx_size):
@@ -375,18 +389,8 @@
     keys, values = key_rows[0], value_rows[0]
     k_prev = shift(keys, "ctx", 1, 0)
     v_prev = shift(values, "ctx", 1, 0)
-    k_far, v_far = [], []
-    k_last, v_last, at = k_prev, v_prev, 1
-    for hop in plan.hops:
-        k_last = shift(k_last, "ctx", hop - at, at)
-        v_last = shift(v_last, "ctx", hop - at, at)
-        at = hop
-        k_far.append(k_last)
-        v_far.append(v_last)
-    if count == 1:
-        k_far, v_far = k_far[0][None], v_far[0][None]
-    else:
-        k_far, v_far = jnp.stack(k_far), jnp.stack(v_far)
+    k_far = far_rows(keys, k_prev, plan.hops)
+    v_far = far_rows(values, v_prev, plan.hops)
 
     def array(*shape, dtype=BF16):
         return jax.ShapeDtypeStruct(shape, dtype)

time: 39 us -> 39.2 us (level)
  starting transfers between devices: 13.8 us -> 18.1 us
  waiting for transfers between devices: 12.7 us -> 8.58 us
    ppermute x0 -> x4, starting transfers between devices: none -> 7.74 us  [the longest x2 6.41 us: two_up(): lax.ppermute(own, axis, [(n, n + 2) for n in range(0, count - 2, 2)])]
    ppermute x8 -> x6, waiting for transfers between devices: 12.7 us -> 8.57 us  [shift(): lax.ppermute(value, axis, [(n, n + steps) for n in range(holders, count)...]
    ppermute x8 -> x6, starting transfers between devices: 13.8 us -> 10.3 us  [shift(): lax.ppermute(value, axis, [(n, n + steps) for n in range(holders, count)...]
  transfers between devices with their start and end apart: 8 -> 10, of which waited for: 3 -> 3; matrix products, arithmetic and copies ran while one was open for 0% -> 0% of each run, Pallas kernels for 27% -> 27%
where the time goes in v2:
time: 39.2 us; the launch traced here: 38.8 us
  starting transfers between devices  18.1 us (46%)
  Pallas kernels  11.2 us (29%)
  waiting for transfers between devices  8.58 us (22%)
  between operations  0.93 us (2%)
    pallas_call x9, Pallas kernels, call(): pl.pallas_call(functools.partial(body, plan), in_specs=places or [vmem] *...  11.2 us
    ppermute x6, starting transfers between devices, shift(): lax.ppermute(value, axis, [(n, n + steps) for n in range(holders, count)...  10.3 us
    ppermute x6, waiting for transfers between devices, shift(): lax.ppermute(value, axis, [(n, n + steps) for n in range(holders, count)...  8.57 us
    ppermute x2, starting transfers between devices, two_up(): lax.ppermute(own, axis, [(n, n + 2) for n in range(0, count - 2, 2)])  6.41 us
    ppermute x2, starting transfers between devices, two_up(): lax.ppermute(near, axis, [(n, n + 1) for n in range(2, count - 1, 2)])  1.33 us
  transfers between devices with their start and end apart: 10, of which 3 were waited for; matrix products, arithmetic and copies ran while one was open for 0% of the time, Pallas kernels for 27%

profile of v2, /device:TPU:0, one launch (start us, length us, event | category | flops | bytes accessed | tf_op | source)
XLA Modules:
  0.0 38.8 jit_solution(3428035619112990581)
XLA Ops:
  0.6 5.0 %collective-permute-start = (bf16[512,128]{1,0:T(8,128)(2,1)}, bf16[512,128]{1,0:T(8,128)(2,1)S(1)}, u32[]{:S(2)}, u32[]{:S(2)}) collective-permute-start(bf16[512,128]{1,0:T(8,128)(2,1)} %bitcast.8), channel_id=1, source_target_pairs={{0,4},{4,8},{8,12},{1,5},{5,9},{9,13},{2,6},{6,10},{10,14},{3,7},{... | collective-permute-start | bytes 393224 | tf_op jit(solution)/shard_map/ppermute | solution.py:25
  5.6 4.5 %collective-permute-start.1 = (bf16[512,128]{1,0:T(8,128)(2,1)}, bf16[512,128]{1,0:T(8,128)(2,1)S(1)}, u32[]{:S(2)}, u32[]{:S(2)}) collective-permute-start(bf16[512,128]{1,0:T(8,128)(2,1)} %bitcast.9), channel_id=1, source_target_pairs={{0,8},{1,9},{2,10},{3,11},{16,24},{17,25},{18,26},{19,27}} | collective-permute-start | bytes 393224 | tf_op jit(solution)/shard_map/ppermute | solution.py:30
  10.1 0.0 copy-start
  10.1 0.0 copy-start.1
  10.1 0.0 copy-start.2
  10.1 0.0 copy-start.3
  10.1 0.0 copy-start.4
  10.2 1.4 %collective-permute-start.4 = (bf16[512,128]{1,0:T(8,128)(2,1)}, bf16[512,128]{1,0:T(8,128)(2,1)S(1)}, u32[]{:S(2)}, u32[]{:S(2)}) collective-permute-start(bf16[512,128]{1,0:T(8,128)(2,1)} %bitcast.11), channel_id=1, source_target_pairs={{0,4},{4,8},{8,12},{1,5},{5,9},{9,13},{2,6},{6,10},{10,14},{3,7},{... | collective-permute-start | bytes 393224 | tf_op jit(solution)/shard_map/ppermute | solution.py:25
  11.6 1.9 %collective-permute-start.3 = (bf16[512,128]{1,0:T(8,128)(2,1)}, bf16[512,128]{1,0:T(8,128)(2,1)S(1)}, u32[]{:S(2)}, u32[]{:S(2)}) collective-permute-start(bf16[512,128]{1,0:T(8,128)(2,1)} %bitcast.12), channel_id=1, source_target_pairs={{0,8},{1,9},{2,10},{3,11},{16,24},{17,25},{18,26},{19,27}} | collective-permute-start | bytes 393224 | tf_op jit(solution)/shard_map/ppermute | solution.py:30
  13.5 0.0 collective-permute-done.k_ref.kp_ref
  13.5 0.7 %collective-permute-start.2 = (bf16[512,128]{1,0:T(8,128)(2,1)S(1)}, bf16[512,128]{1,0:T(8,128)(2,1)S(1)}, u32[]{:S(2)}, u32[]{:S(2)}) collective-permute-start(bf16[512,128]{1,0:T(8,128)(2,1)S(1)} %collective-permute-done.k_ref.kp_ref), channel_id=1, source_target_pairs={{8,12},{9,13},{10,14},{11,15},{24,28},{25,29},{26,30},{27,31}} | collective-permute-start | bytes 393224 | tf_op jit(solution)/shard_map/ppermute | solution.py:31
  14.3 0.0 copy-done
  14.3 0.0 copy-done.1
  14.3 0.0 copy-done.2
  14.3 0.0 copy-done.3
  14.3 0.0 copy-done.4
  14.3 2.3 %shard_map.85 = (f32[4,16,1024]{2,1,0:T(8,128)S(1)}, f32[4,8,1024]{2,1,0:T(8,128)S(1)}, f32[4,136,1024]{2,1,0:T(8,128)S(1)}, bf16[1152,1024]{1,0:T(8,128)(2,1)S(1)}, bf16[4,128,1024]{2,1,0:T(8,128)(2,1)S(1)}) custom-call(s32[4,11]{1,0:T(4,128)S(1)} %copy-done.4, f32[128,1024]{1,0:T(8,128)S(1)} %shard_map.84.causal_ref, bf16[8,512,128]{2,1,0:T(8,128)(2,1)S(1)} %copy-done, ...), custom_call_target="tpu_custom_call" | custom-call | flops 603979776 | bytes 2097152 | tf_op jit(solution)/shard_map/pallas_call | solution.py:404
  16.6 0.5 %collective-permute-done.4.v_ref = bf16[512,128]{1,0:T(8,128)(2,1)S(1)} collective-permute-done((bf16[512,128]{1,0:T(8,128)(2,1)}, bf16[512,128]{1,0:T(8,128)(2,1)S(1)}, u32[]{:S(2)}, u32[]{:S(2)}) %collective-permute-start.4) | collective-permute-done | bytes 131104 | tf_op jit(solution)/shard_map/ppermute | solution.py:25
  17.0 0.7 %collective-permute-start.5 = (bf16[512,128]{1,0:T(8,128)(2,1)S(1)}, bf16[512,128]{1,0:T(8,128)(2,1)S(1)}, u32[]{:S(2)}, u32[]{:S(2)}) collective-permute-start(bf16[512,128]{1,0:T(8,128)(2,1)S(1)} %collective-permute-done.4.v_ref), channel_id=1, source_target_pairs={{8,12},{9,13},{10,14},{11,15},{24,28},{25,29},{26,30},{27,31}} | collective-permute-start | bytes 393224 | tf_op jit(solution)/shard_map/ppermute | solution.py:31
  17.7 1.7 %shard_map.86 = (f32[4,8,1024]{2,1,0:T(8,128)S(1)}, f32[4,136,1024]{2,1,0:T(8,128)S(1)}, bf16[896,1024]{1,0:T(8,128)(2,1)S(1)}) custom-call(bf16[8,512,128]{2,1,0:T(8,128)(2,1)S(1)} %copy-done, bf16[512,128]{1,0:T(8,128)(2,1)S(1)} %collective-permute-done.k_ref.kp_ref, bf16[512,128]{1,0:T(8,128)(2,1)S(1)} %collective-permute-done.4.v_ref, ...), custom_call_target="tpu_custom_call" | custom-call | flops 469762048 | bytes 2097152 | tf_op jit(solution)/shard_map/pallas_call | solution.py:404
  19.4 0.0 collective-permute-done.1
  19.4 0.0 collective-permute-done.2
  19.4 0.1 shard_map.87
  19.5 0.7 %collective-permute-start.8 = (bf16[512,128]{1,0:T(8,128)(2,1)S(1)}, bf16[512,128]{1,0:T(8,128)(2,1)S(1)}, u32[]{:S(2)}, u32[]{:S(2)}) collective-permute-start(bf16[512,128]{1,0:T(8,128)(2,1)S(1)} %bitcast.14), channel_id=1, source_target_pairs={{8,4},{12,8},{9,5},{13,9},{10,6},{14,10},{11,7},{15,11},{24,20},{2... | collective-permute-start | bytes 393224 | tf_op jit(solution)/shard_map/ppermute | solution.py:25
  20.2 0.0 collective-permute-done.3
  20.2 0.0 collective-permute-done.5
  20.2 0.1 shard_map.88
  20.4 0.7 %collective-permute-start.6 = (bf16[512,128]{1,0:T(8,128)(2,1)S(1)}, bf16[512,128]{1,0:T(8,128)(2,1)S(1)}, u32[]{:S(2)}, u32[]{:S(2)}) collective-permute-start(bf16[512,128]{1,0:T(8,128)(2,1)S(1)} %bitcast.15), channel_id=1, source_target_pairs={{8,4},{12,8},{9,5},{13,9},{10,6},{14,10},{11,7},{15,11},{24,20},{2... | collective-permute-start | bytes 393224 | tf_op jit(solution)/shard_map/ppermute | solution.py:25
  21.0 0.7 %shard_map.89 = (f32[512,128]{1,0:T(8,128)S(1)}, bf16[4,128,1024]{2,1,0:T(8,128)(2,1)S(1)}) custom-call(bf16[4,128,1024]{2,1,0:T(8,128)(2,1)S(1)} %get-tuple-element.28.dot_ref, f32[4,8,1024]{2,1,0:T(8,128)S(1)} %get-tuple-element.36.fin_ref, bf16[896,1024]{1,0:T(8,128)(2,1)S(1)} %get-tuple-element.38.p_ref), custom_call_target="tpu_custom_call" | custom-call | flops 234881024 | bytes 2097152 | tf_op jit(solution)/shard_map/pallas_call | solution.py:404
  21.7 1.3 %shard_map.90 = (f32[512,128]{1,0:T(8,128)S(1)}, bf16[896,1024]{1,0:T(8,128)(2,1)S(1)}) custom-call(bf16[8,512,128]{2,1,0:T(8,128)(2,1)S(1)} %copy-done, bf16[512,128]{1,0:T(8,128)(2,1)S(1)} %collective-permute-done.4.v_ref, f32[4,8,1024]{2,1,0:T(8,128)S(1)} %get-tuple-element.36.fin_ref, bf16[896,1024]{1,0:T(8,128)(2,1)S(1)} %get-tuple-element.38.p_ref, ...), custom_call_target="tpu_custom_call" | custom-call | flops 469762048 | bytes 2097152 | tf_op jit(solution)/shard_map/pallas_call | solution.py:404
  23.0 0.0 collective-permute-done.8
  23.0 1.3 %collective-permute-start.9 = (bf16[512,128]{1,0:T(8,128)(2,1)S(1)}, bf16[512,128]{1,0:T(8,128)(2,1)S(1)}, u32[]{:S(2)}, u32[]{:S(2)}) collective-permute-start(bf16[512,128]{1,0:T(8,128)(2,1)S(1)} %add_convert_fusion), channel_id=1, source_target_pairs={{4,0},{8,4},{12,8},{5,1},{9,5},{13,9},{6,2},{10,6},{14,10},{7,3},{... | collective-permute-start | bytes 393224 | tf_op jit(solution)/shard_map/ppermute | solution.py:25
  24.3 0.0 collective-permute-done.6
  24.4 1.3 %collective-permute-start.7 = (bf16[512,128]{1,0:T(8,128)(2,1)S(1)}, bf16[512,128]{1,0:T(8,128)(2,1)S(1)}, u32[]{:S(2)}, u32[]{:S(2)}) collective-permute-start(bf16[512,128]{1,0:T(8,128)(2,1)S(1)} %add_convert_fusion.1), channel_id=1, source_target_pairs={{4,0},{8,4},{12,8},{5,1},{9,5},{13,9},{6,2},{10,6},{14,10},{7,3},{... | collective-permute-start | bytes 393224 | tf_op jit(solution)/shard_map/ppermute | solution.py:25
  25.7 4.3 %shard_map.91 = (f32[512,128]{1,0:T(8,128)S(1)}, f32[512,128]{1,0:T(8,128)S(1)}, bf16[8,512,128]{2,1,0:T(8,128)(2,1)}, bf16[8,512,128]{2,1,0:T(8,128)(2,1)}) custom-call(bf16[8,512,128]{2,1,0:T(8,128)(2,1)S(1)} %copy-done, bf16[4,128,1024]{2,1,0:T(8,128)(2,1)S(1)} %get-tuple-element.28.dot_ref, bf16[512,128]{1,0:T(8,128)(2,1)S(1)} %bitcast.10, ...), custom_call_target="tpu_custom_call" | custom-call | flops 1509949440 | bytes 2097152 | tf_op jit(solution)/shard_map/pallas_call | solution.py:404
  30.0 5.3 %collective-permute-done.9.vg_ref = bf16[512,128]{1,0:T(8,128)(2,1)S(1)} collective-permute-done((bf16[512,128]{1,0:T(8,128)(2,1)S(1)}, bf16[512,128]{1,0:T(8,128)(2,1)S(1)}, u32[]{:S(2)}, u32[]{:S(2)}) %collective-permute-start.9) | collective-permute-done | bytes 131104 | tf_op jit(solution)/shard_map/ppermute | solution.py:25
  35.3 2.8 %collective-permute-done.7.kg_ref = bf16[512,128]{1,0:T(8,128)(2,1)S(1)} collective-permute-done((bf16[512,128]{1,0:T(8,128)(2,1)S(1)}, bf16[512,128]{1,0:T(8,128)(2,1)S(1)}, u32[]{:S(2)}, u32[]{:S(2)}) %collective-permute-start.7) | collective-permute-done | bytes 131104 | tf_op jit(solution)/shard_map/ppermute | solution.py:25
  38.1 0.7 %shard_map.92 = (bf16[1,512,128]{2,1,0:T(8,128)(2,1)}, bf16[1,512,128]{2,1,0:T(8,128)(2,1)}) custom-call(f32[512,128]{1,0:T(8,128)S(1)} %get-tuple-element.44.dk_ref, f32[512,128]{1,0:T(8,128)S(1)} %get-tuple-element.45.dv_ref, bf16[512,128]{1,0:T(8,128)(2,1)S(1)} %collective-permute-done.7.kg_ref, bf16[512,128]{1,0:T(8,128)(2,1)S(1)} %collective-permute-done.9.vg_ref), custom_call_target="tpu_custom_call" | custom-call | flops 33554432 | bytes 2097152 | tf_op jit(solution)/shard_map/pallas_call | solution.py:404
  (5 shorter events, 0.1 us)
Async XLA Ops:
  0.6 12.9 %collective-permute-start = (bf16[512,128]{1,0:T(8,128)(2,1)}, bf16[512,128]{1,0:T(8,128)(2,1)S(1)}, u32[]{:S(2)}, u32[]{:S(2)}) collective-permute-start(bf16[512,128]{1,0:T(8,128)(2,1)} %bitcast.8), channel_id=1, source_target_pairs={{0,4},{4,8},{8,12},{1,5},{5,9},{9,13},{2,6},{6,10},{10,14},{3,7},{... | collective-permute-start | bytes 393224 | tf_op jit(solution)/shard_map/ppermute | solution.py:25
  5.6 13.8 %collective-permute-start.1 = (bf16[512,128]{1,0:T(8,128)(2,1)}, bf16[512,128]{1,0:T(8,128)(2,1)S(1)}, u32[]{:S(2)}, u32[]{:S(2)}) collective-permute-start(bf16[512,128]{1,0:T(8,128)(2,1)} %bitcast.9), channel_id=1, source_target_pairs={{0,8},{1,9},{2,10},{3,11},{16,24},{17,25},{18,26},{19,27}} | collective-permute-start | bytes 393224 | tf_op jit(solution)/shard_map/ppermute | solution.py:30
  10.1 4.1 %copy-start = (bf16[8,512,128]{2,1,0:T(8,128)(2,1)S(1)}, bf16[8,512,128]{2,1,0:T(8,128)(2,1)}, u32[]{:S(2)}) copy-start(bf16[8,512,128]{2,1,0:T(8,128)(2,1)} %q_ref.11) | copy-start | bytes 3145732
  10.1 4.1 %copy-start.1 = (bf16[8,512,128]{2,1,0:T(8,128)(2,1)S(1)}, bf16[8,512,128]{2,1,0:T(8,128)(2,1)}, u32[]{:S(2)}) copy-start(bf16[8,512,128]{2,1,0:T(8,128)(2,1)} %do_ref.1) | copy-start | bytes 3145732
  10.1 4.1 %copy-start.2 = (bf16[1,512,128]{2,1,0:T(8,128)(2,1)S(1)}, bf16[1,512,128]{2,1,0:T(8,128)(2,1)}, u32[]{:S(2)}) copy-start(bf16[1,512,128]{2,1,0:T(8,128)(2,1)} %k_ref.1) | copy-start | bytes 393220
  10.1 4.1 %copy-start.3 = (bf16[1,512,128]{2,1,0:T(8,128)(2,1)S(1)}, bf16[1,512,128]{2,1,0:T(8,128)(2,1)}, u32[]{:S(2)}) copy-start(bf16[1,512,128]{2,1,0:T(8,128)(2,1)} %v_ref.1) | copy-start | bytes 393220
  10.1 4.1 %copy-start.4 = (s32[4,11]{1,0:T(4,128)S(1)}, s32[4,11]{1,0:T(4,128)}, u32[]{:S(2)}) copy-start(s32[4,11]{1,0:T(4,128)} %link_ref.1) | copy-start | bytes 532
  10.2 6.9 %collective-permute-start.4 = (bf16[512,128]{1,0:T(8,128)(2,1)}, bf16[512,128]{1,0:T(8,128)(2,1)S(1)}, u32[]{:S(2)}, u32[]{:S(2)}) collective-permute-start(bf16[512,128]{1,0:T(8,128)(2,1)} %bitcast.11), channel_id=1, source_target_pairs={{0,4},{4,8},{8,12},{1,5},{5,9},{9,13},{2,6},{6,10},{10,14},{3,7},{... | collective-permute-start | bytes 393224 | tf_op jit(solution)/shard_map/ppermute | solution.py:25
  11.6 8.6 %collective-permute-start.3 = (bf16[512,128]{1,0:T(8,128)(2,1)}, bf16[512,128]{1,0:T(8,128)(2,1)S(1)}, u32[]{:S(2)}, u32[]{:S(2)}) collective-permute-start(bf16[512,128]{1,0:T(8,128)(2,1)} %bitcast.12), channel_id=1, source_target_pairs={{0,8},{1,9},{2,10},{3,11},{16,24},{17,25},{18,26},{19,27}} | collective-permute-start | bytes 393224 | tf_op jit(solution)/shard_map/ppermute | solution.py:30
  13.5 5.8 %collective-permute-start.2 = (bf16[512,128]{1,0:T(8,128)(2,1)S(1)}, bf16[512,128]{1,0:T(8,128)(2,1)S(1)}, u32[]{:S(2)}, u32[]{:S(2)}) collective-permute-start(bf16[512,128]{1,0:T(8,128)(2,1)S(1)} %collective-permute-done.k_ref.kp_ref), channel_id=1, source_target_pairs={{8,12},{9,13},{10,14},{11,15},{24,28},{25,29},{26,30},{27,31}} | collective-permute-start | bytes 393224 | tf_op jit(solution)/shard_map/ppermute | solution.py:31
  17.0 3.2 %collective-permute-start.5 = (bf16[512,128]{1,0:T(8,128)(2,1)S(1)}, bf16[512,128]{1,0:T(8,128)(2,1)S(1)}, u32[]{:S(2)}, u32[]{:S(2)}) collective-permute-start(bf16[512,128]{1,0:T(8,128)(2,1)S(1)} %collective-permute-done.4.v_ref), channel_id=1, source_target_pairs={{8,12},{9,13},{10,14},{11,15},{24,28},{25,29},{26,30},{27,31}} | collective-permute-start | bytes 393224 | tf_op jit(solution)/shard_map/ppermute | solution.py:31
  19.5 3.4 %collective-permute-start.8 = (bf16[512,128]{1,0:T(8,128)(2,1)S(1)}, bf16[512,128]{1,0:T(8,128)(2,1)S(1)}, u32[]{:S(2)}, u32[]{:S(2)}) collective-permute-start(bf16[512,128]{1,0:T(8,128)(2,1)S(1)} %bitcast.14), channel_id=1, source_target_pairs={{8,4},{12,8},{9,5},{13,9},{10,6},{14,10},{11,7},{15,11},{24,20},{2... | collective-permute-start | bytes 393224 | tf_op jit(solution)/shard_map/ppermute | solution.py:25
  20.4 4.0 %collective-permute-start.6 = (bf16[512,128]{1,0:T(8,128)(2,1)S(1)}, bf16[512,128]{1,0:T(8,128)(2,1)S(1)}, u32[]{:S(2)}, u32[]{:S(2)}) collective-permute-start(bf16[512,128]{1,0:T(8,128)(2,1)S(1)} %bitcast.15), channel_id=1, source_target_pairs={{8,4},{12,8},{9,5},{13,9},{10,6},{14,10},{11,7},{15,11},{24,20},{2... | collective-permute-start | bytes 393224 | tf_op jit(solution)/shard_map/ppermute | solution.py:25
  23.0 12.2 %collective-permute-start.9 = (bf16[512,128]{1,0:T(8,128)(2,1)S(1)}, bf16[512,128]{1,0:T(8,128)(2,1)S(1)}, u32[]{:S(2)}, u32[]{:S(2)}) collective-permute-start(bf16[512,128]{1,0:T(8,128)(2,1)S(1)} %add_convert_fusion), channel_id=1, source_target_pairs={{4,0},{8,4},{12,8},{5,1},{9,5},{13,9},{6,2},{10,6},{14,10},{7,3},{... | collective-permute-start | bytes 393224 | tf_op jit(solution)/shard_map/ppermute | solution.py:25
  24.4 13.7 %collective-permute-start.7 = (bf16[512,128]{1,0:T(8,128)(2,1)S(1)}, bf16[512,128]{1,0:T(8,128)(2,1)S(1)}, u32[]{:S(2)}, u32[]{:S(2)}) collective-permute-start(bf16[512,128]{1,0:T(8,128)(2,1)S(1)} %add_convert_fusion.1), channel_id=1, source_target_pairs={{4,0},{8,4},{12,8},{5,1},{9,5},{13,9},{6,2},{10,6},{14,10},{7,3},{... | collective-permute-start | bytes 393224 | tf_op jit(solution)/shard_map/ppermute | solution.py:25

commit v3 on v2

--- a/solution.py
+++ b/solution.py
@@ -11,8 +11,10 @@
 
 BLK = 128
 NOFF = 11
-WIDE = 8
-FAR_WIDE = 8
+OWN_WIDE = 8
+PREV_WIDE = 4
+SCORE_WIDE = 2
+KEY_WIDE = 4
 BACK_WIDE = 2
 NEG = -1e30
 LOG2E = 1.4426950408889634
@@ -117,14 +119,14 @@
     return exps, top
 
 
-def staged(items, first, second):
+def staged(items, *stages):
     items = list(items)
-    ahead = first(items[0])
-    for n, item in enumerate(items):
-        now = ahead
-        if n + 1 < len(items):
-            ahead = first(items[n + 1])
-        second(item, now)
+    held = {}
+    for step in range(len(items) + len(stages) - 1):
+        for k, stage in enumerate(stages):
+            n = step - k
+            if 0 <= n < len(items):
+                held[n] = stage(items[n], *held.pop(n, ()))
 
 
 def causal_mask(plan, mask_ref):
@@ -134,7 +136,7 @@
 
 
 def local_forward(
-    plan, link_ref, causal_ref, q_ref, do_ref, k_ref, v_ref, bias_ref, stat_ref, acc_ref, p_ref, dot_ref
+    plan, link_ref, causal_ref, q_ref, do_ref, k_ref, v_ref, bias_ref, stat_ref, acc_ref, p_ref, dot_ref, qt_ref
 ):
     first_block = lax.axis_index("ctx") * plan.blocks
     scalars = []
@@ -150,22 +152,28 @@
     def first(item):
         i, heads, _ = item
         keys = stack([k_ref[0, block(b)] for _, b in plan.own[i]])
-        return dot_nt(keys, rows_of(q_ref, heads, i, size))
+        return (dot_nt(keys, rows_of(q_ref, heads, i, size)),)
 
     def second(item, raw):
-        i, heads, lanes = item
+        i, _, lanes = item
         slots = plan.own[i]
-        vt = stack([values_t[:, block(b)] for _, b in slots], axis=1)
         biases = [scalars[i][n] if plan.entries[n][1] > 0 else None for n, _ in slots]
         at = plan.own_at[i] * BLK
         exps, top = scores_of(plan, raw, biases, causal_ref[:, lanes], None)
         low = stack([part.astype(BF16) for part in exps])
         p_ref[at : at + low.shape[0], lanes] = low
         stat_ref[i, 0:1, lanes] = top
+        return (low,)
+
+    def third(item, low):
+        i, heads, lanes = item
+        vt = stack([values_t[:, block(b)] for _, b in plan.own[i]], axis=1)
         acc_ref[i, :, lanes] = dot_nn(vt, low)[: size + 8]
         dot_ref[i, :, lanes] = rows_of(do_ref, heads, i, size).T
-
-    staged(plan.items(WIDE), first, second)
+        qt_ref[i, :, lanes] = rows_of(q_ref, heads, i, size).T
+        return ()
+
+    staged(plan.items(OWN_WIDE), first, second, third)
 
 
 def prev_forward(plan, q_ref, k_ref, v_ref, dot_ref, bias_ref, stat_in, acc_in, stat_ref, acc_ref, p_ref):
@@ -175,25 +183,30 @@
     def first(item):
         i, heads, _ = item
         keys = stack([k_ref[block(b)] for _, b in plan.prev[i]])
-        return dot_nt(keys, rows_of(q_ref, heads, i, size))
+        return (dot_nt(keys, rows_of(q_ref, heads, i, size)),)
 
     def second(item, raw):
         i, _, lanes = item
         slots = plan.prev[i]
-        vt = stack([values_t[:, block(b)] for _, b in slots], axis=1)
         at = plan.prev_at[i] * BLK
         before = stat_in[i, 0:1, lanes]
         biases = [bias_ref[i, n : n + 1, lanes] for n, _ in slots]
         exps, top = scores_of(plan, raw, biases, None, before)
         low = stack([part.astype(BF16) for part in exps])
         p_ref[at : at + low.shape[0], lanes] = low
+        return low, before, top
+
+    def third(item, low, before, top):
+        i, _, lanes = item
+        vt = stack([values_t[:, block(b)] for _, b in plan.prev[i]], axis=1)
         acc = acc_in[i, :, lanes] * jnp.exp2(before - top) + dot_nn(vt, low)[: size + 8]
         acc_ref[i, :, lanes] = acc
         stat_ref[i, 0:1, lanes] = before
         stat_ref[i, 1:2, lanes] = top
         stat_ref[i, 2:3, lanes] = jnp.sum(acc[:size] * dot_ref[i, :, lanes].astype(F32), axis=0, keepdims=True)
-
-    staged(plan.items(WIDE), first, second)
+        return ()
+
+    staged(plan.items(PREV_WIDE), first, second, third)
 
 
 def has_far(plan):
@@ -207,7 +220,7 @@
     def first(item):
         i, heads, _ = item
         keys = stack([k_ref[f, block(i)] for f in range(count)])
-        return dot_nt(keys, rows_of(q_ref, heads, i, size))
+        return (dot_nt(keys, rows_of(q_ref, heads, i, size)),)
 
     def second(item, raw):
         i, _, lanes = item
@@ -222,14 +235,19 @@
         fin_ref[i, 0:1, lanes] = jnp.exp2(stat_ref[i, 0:1, lanes] - top) * inverse
         fin_ref[i, 1:2, lanes] = fade * inverse
         fin_ref[i, 2:3, lanes] = stat_ref[i, 2:3, lanes] * (fade * inverse)
+        return ()
+
+    def third(item):
+        i, _, lanes = item
         if lanes.stop == plan.lanes:
             dv = dot_nt(low_ref[i], dot_ref[i])
             for f in range(count):
                 dv_ref[f, block(i)] = dv[block(f)].astype(BF16)
+        return ()
 
     @pl.when(has_far(plan))
     def _():
-        staged(plan.items(FAR_WIDE), first, second)
+        staged(plan.items(SCORE_WIDE), first, second, third)
 
     @pl.when(jnp.logical_not(has_far(plan)))
     def _():
@@ -242,14 +260,13 @@
             fin_ref[i, 2:3, :] = stat_ref[i, 2:3, :] * inverse
 
 
-def far_keys(plan, q_ref, dot_ref, v_ref, low_ref, fin_in, dk_ref, ds_ref, fin_ref):
-    size = plan.size
+def far_keys(plan, qt_ref, dot_ref, v_ref, low_ref, fin_in, dk_ref, ds_ref, fin_ref):
     count = len(plan.far)
 
     def first(item):
         i, _, lanes = item
         values = stack([v_ref[f, block(i)] for f in range(count)])
-        return dot_nn(values, dot_ref[i, :, lanes])
+        return (dot_nn(values, dot_ref[i, :, lanes]),)
 
     def second(item, grad_w):
         i, _, lanes = item
@@ -258,16 +275,21 @@
         row_dot = fin_in[i, 2:3, lanes] + jnp.sum(products, axis=0, keepdims=True)
         ds_ref[i, :, lanes] = (products - weights * row_dot).astype(BF16)
         fin_ref[i, 2:3, lanes] = row_dot
+        return ()
+
+    def third(item):
+        i, _, lanes = item
         if lanes.stop == plan.lanes:
-            dk = dot_nn(ds_ref[i], rows_of(q_ref, slice(0, plan.heads), i, size)) * plan.inv_root
+            dk = dot_nt(ds_ref[i], qt_ref[i]) * plan.inv_root
             for f in range(count):
                 dk_ref[f, block(i)] = dk[block(f)].astype(BF16)
+        return ()
 
     fin_ref[...] = fin_in[...]
 
     @pl.when(has_far(plan))
     def _():
-        staged(plan.items(FAR_WIDE), first, second)
+        staged(plan.items(KEY_WIDE), first, second, third)
 
     @pl.when(jnp.logical_not(has_far(plan)))
     def _():
@@ -305,21 +327,21 @@
         dv_ref[block(b)] = sums[b]
 
 
-def prev_keys(plan, q_ref, v_ref, fin_ref, p_ref, scaled_ref, dk_ref, ds_ref):
+def prev_keys(plan, qt_ref, v_ref, fin_ref, p_ref, scaled_ref, dk_ref, ds_ref):
     sums = {}
     for i in range(plan.blocks):
         slots = plan.prev[i]
         values = stack([v_ref[block(b)] for _, b in slots])
         at, end = plan.prev_at[i] * BLK, plan.prev_at[i + 1] * BLK
         score_grads(plan, i, slots, values, 1, fin_ref, p_ref, at, ds_ref, at, scaled_ref)
-        dk = dot_nn(ds_ref[at:end, :], rows_of(q_ref, slice(0, plan.heads), i, plan.size))
+        dk = dot_nt(ds_ref[at:end, :], qt_ref[i])
         add_blocks(sums, slots, dk)
     for b in range(plan.blocks):
         dk_ref[block(b)] = sums[b] * plan.inv_root
 
 
 def local_backward(
-    plan, q_ref, dot_ref, k_ref, v_ref, kp_ref, kf_ref, vf_ref, fin_ref, acc_ref, low_ref, p_ref, dsp_ref, dsf_ref,
+    plan, qt_ref, dot_ref, k_ref, v_ref, kp_ref, kf_ref, vf_ref, fin_ref, acc_ref, low_ref, p_ref, dsp_ref, dsf_ref,
     dk_ref, dv_ref, o_hbm, dq_hbm, scaled_ref, ds_ref, o_ref, dq_ref, sems,
 ):
     size = plan.size
@@ -358,8 +380,10 @@
             dq_t = (dot_nn(kt, stack(ds)) * plan.inv_root).astype(BF16)
             dq_ref[heads, block(i)] = dq_t.T.reshape(BACK_WIDE, BLK, size)
         send(dq_ref, dq_hbm, i)
-        add_blocks(dv_sums, slots, dot_nt(p_ref[at:end, :], scaled_ref[i]))
-        add_blocks(dk_sums, slots, dot_nn(ds_ref[at:end, :], rows_of(q_ref, slice(0, plan.heads), i, size)))
+    for i in range(plan.blocks):
+        at, end = plan.own_at[i] * BLK, plan.own_at[i + 1] * BLK
+        add_blocks(dv_sums, plan.own[i], dot_nt(p_ref[at:end, :], scaled_ref[i]))
+        add_blocks(dk_sums, plan.own[i], dot_nt(ds_ref[at:end, :], qt_ref[i]))
     for b in range(plan.blocks):
         dk_ref[block(b)] = dk_sums[b] * plan.inv_root
         dv_ref[block(b)] = dv_sums[b]
@@ -427,9 +451,9 @@
     whole = pltpu.VMEM(queries.shape, BF16)
 
     causal = call(causal_mask, n_own, 8, [array(BLK, lanes, dtype=F32)], ())[0]
-    bias, stat_own, acc_own, p_own, grad_t = call(
+    bias, stat_own, acc_own, p_own, grad_t, query_t = call(
         local_forward, n_own, 2,
-        [bias, stat, acc, own_shape, grads_t],
+        [bias, stat, acc, own_shape, grads_t, grads_t],
         (link_mask, causal, queries, out_grad, key_rows, value_rows),
         places=[smem] + [vmem] * 5,
     )
@@ -446,14 +470,14 @@
     dk_far, ds_far, fin = call(
         far_keys, n_far, 2,
         [far_shape, ds_shape, stat],
-        (queries, grad_t, v_far, low_far, fin),
+        (query_t, grad_t, v_far, low_far, fin),
     )
     dv_prev, scaled = call(prev_values, n_prev, 1, [total, grads_t], (grad_t, fin, p_prev))
-    dk_prev, ds_prev = call(prev_keys, n_prev, 2, [total, prev_shape], (queries, v_prev, fin, p_prev, scaled))
+    dk_prev, ds_prev = call(prev_keys, n_prev, 2, [total, prev_shape], (query_t, v_prev, fin, p_prev, scaled))
     dk_own, dv_own, output, query_grad = call(
         local_backward, n_own, 5,
         [total, total, full, full],
-        (queries, grad_t, keys, values, k_prev, k_far, v_far, fin, acc_near, low_far, p_own, ds_prev, ds_far),
+        (query_t, grad_t, keys, values, k_prev, k_far, v_far, fin, acc_near, low_far, p_own, ds_prev, ds_far),
         scratch=[
             pltpu.VMEM(grads_t.shape, BF16), pltpu.VMEM(own_shape.shape, BF16), whole, whole, pltpu.SemaphoreType.DMA((2 * blocks,))
         ],

time: 39.2 us -> 38.9 us (level)
  no operation moved by 1% of the time
where the time goes in v3:
time: 38.9 us; the launch traced here: 38.6 us
  starting transfers between devices  18.1 us (47%)
  Pallas kernels  11.1 us (29%)
  waiting for transfers between devices  8.38 us (22%)
  between operations  0.93 us (2%)
    pallas_call x9, Pallas kernels, call(): pl.pallas_call(functools.partial(body, plan), in_specs=places or [vmem] *...  11.1 us
    ppermute x6, starting transfers between devices, shift(): lax.ppermute(value, axis, [(n, n + steps) for n in range(holders, count)...  10.3 us
    ppermute x6, waiting for transfers between devices, shift(): lax.ppermute(value, axis, [(n, n + steps) for n in range(holders, count)...  8.36 us
    ppermute x2, starting transfers between devices, two_up(): lax.ppermute(own, axis, [(n, n + 2) for n in range(0, count - 2, 2)])  6.41 us
    ppermute x2, starting transfers between devices, two_up(): lax.ppermute(near, axis, [(n, n + 1) for n in range(2, count - 1, 2)])  1.33 us
  transfers between devices with their start and end apart: 10, of which 3 were waited for; matrix products, arithmetic and copies ran while one was open for 0% of the time, Pallas kernels for 27%

profile of v3, /device:TPU:0, one launch (start us, length us, event | category | flops | bytes accessed | tf_op | source)
XLA Modules:
  0.0 38.6 jit_solution(6054101694629582468)
XLA Ops:
  0.6 5.0 %collective-permute-start = (bf16[512,128]{1,0:T(8,128)(2,1)}, bf16[512,128]{1,0:T(8,128)(2,1)S(1)}, u32[]{:S(2)}, u32[]{:S(2)}) collective-permute-start(bf16[512,128]{1,0:T(8,128)(2,1)} %bitcast.8), channel_id=1, source_target_pairs={{0,4},{4,8},{8,12},{1,5},{5,9},{9,13},{2,6},{6,10},{10,14},{3,7},{... | collective-permute-start | bytes 393224 | tf_op jit(solution)/shard_map/ppermute | solution.py:27
  5.6 4.5 %collective-permute-start.1 = (bf16[512,128]{1,0:T(8,128)(2,1)}, bf16[512,128]{1,0:T(8,128)(2,1)S(1)}, u32[]{:S(2)}, u32[]{:S(2)}) collective-permute-start(bf16[512,128]{1,0:T(8,128)(2,1)} %bitcast.9), channel_id=1, source_target_pairs={{0,8},{1,9},{2,10},{3,11},{16,24},{17,25},{18,26},{19,27}} | collective-permute-start | bytes 393224 | tf_op jit(solution)/shard_map/ppermute | solution.py:32
  10.1 0.0 copy-start
  10.1 0.0 copy-start.1
  10.1 0.0 copy-start.2
  10.1 0.0 copy-start.3
  10.1 0.0 copy-start.4
  10.2 1.4 %collective-permute-start.4 = (bf16[512,128]{1,0:T(8,128)(2,1)}, bf16[512,128]{1,0:T(8,128)(2,1)S(1)}, u32[]{:S(2)}, u32[]{:S(2)}) collective-permute-start(bf16[512,128]{1,0:T(8,128)(2,1)} %bitcast.11), channel_id=1, source_target_pairs={{0,4},{4,8},{8,12},{1,5},{5,9},{9,13},{2,6},{6,10},{10,14},{3,7},{... | collective-permute-start | bytes 393224 | tf_op jit(solution)/shard_map/ppermute | solution.py:27
  11.6 1.9 %collective-permute-start.3 = (bf16[512,128]{1,0:T(8,128)(2,1)}, bf16[512,128]{1,0:T(8,128)(2,1)S(1)}, u32[]{:S(2)}, u32[]{:S(2)}) collective-permute-start(bf16[512,128]{1,0:T(8,128)(2,1)} %bitcast.12), channel_id=1, source_target_pairs={{0,8},{1,9},{2,10},{3,11},{16,24},{17,25},{18,26},{19,27}} | collective-permute-start | bytes 393224 | tf_op jit(solution)/shard_map/ppermute | solution.py:32
  13.5 0.0 collective-permute-done.k_ref.kp_ref
  13.5 0.7 %collective-permute-start.2 = (bf16[512,128]{1,0:T(8,128)(2,1)S(1)}, bf16[512,128]{1,0:T(8,128)(2,1)S(1)}, u32[]{:S(2)}, u32[]{:S(2)}) collective-permute-start(bf16[512,128]{1,0:T(8,128)(2,1)S(1)} %collective-permute-done.k_ref.kp_ref), channel_id=1, source_target_pairs={{8,12},{9,13},{10,14},{11,15},{24,28},{25,29},{26,30},{27,31}} | collective-permute-start | bytes 393224 | tf_op jit(solution)/shard_map/ppermute | solution.py:33
  14.3 0.0 copy-done
  14.3 0.0 copy-done.1
  14.3 0.0 copy-done.2
  14.3 0.0 copy-done.3
  14.3 0.0 copy-done.4
  14.3 2.3 %shard_map.85 = (f32[4,16,1024]{2,1,0:T(8,128)S(1)}, f32[4,8,1024]{2,1,0:T(8,128)S(1)}, f32[4,136,1024]{2,1,0:T(8,128)S(1)}, bf16[1152,1024]{1,0:T(8,128)(2,1)S(...) custom-call(s32[4,11]{1,0:T(4,128)S(1)} %copy-done.4, f32[128,1024]{1,0:T(8,128)S(1)} %shard_map.84.causal_ref, ...), custom_call_target="tpu_custom_call" | custom-call | flops 603979776 | bytes 2097152 | tf_op jit(solution)/shard_map/pallas_call | solution.py:428
  16.6 0.4 %collective-permute-done.4.v_ref = bf16[512,128]{1,0:T(8,128)(2,1)S(1)} collective-permute-done((bf16[512,128]{1,0:T(8,128)(2,1)}, bf16[512,128]{1,0:T(8,128)(2,1)S(1)}, u32[]{:S(2)}, u32[]{:S(2)}) %collective-permute-start.4) | collective-permute-done | bytes 131104 | tf_op jit(solution)/shard_map/ppermute | solution.py:27
  17.0 0.7 %collective-permute-start.5 = (bf16[512,128]{1,0:T(8,128)(2,1)S(1)}, bf16[512,128]{1,0:T(8,128)(2,1)S(1)}, u32[]{:S(2)}, u32[]{:S(2)}) collective-permute-start(bf16[512,128]{1,0:T(8,128)(2,1)S(1)} %collective-permute-done.4.v_ref), channel_id=1, source_target_pairs={{8,12},{9,13},{10,14},{11,15},{24,28},{25,29},{26,30},{27,31}} | collective-permute-start | bytes 393224 | tf_op jit(solution)/shard_map/ppermute | solution.py:33
  17.7 1.6 %shard_map.86 = (f32[4,8,1024]{2,1,0:T(8,128)S(1)}, f32[4,136,1024]{2,1,0:T(8,128)S(1)}, bf16[896,1024]{1,0:T(8,128)(2,1)S(1)}) custom-call(bf16[8,512,128]{2,1,0:T(8,128)(2,1)S(1)} %copy-done, bf16[512,128]{1,0:T(8,128)(2,1)S(1)} %collective-permute-done.k_ref.kp_ref, bf16[512,128]{1,0:T(8,128)(2,1)S(1)} %collective-permute-done.4.v_ref, ...), custom_call_target="tpu_custom_call" | custom-call | flops 469762048 | bytes 2097152 | tf_op jit(solution)/shard_map/pallas_call | solution.py:428
  19.3 0.0 collective-permute-done.1
  19.4 0.0 collective-permute-done.2
  19.4 0.1 shard_map.87
  19.5 0.7 %collective-permute-start.8 = (bf16[512,128]{1,0:T(8,128)(2,1)S(1)}, bf16[512,128]{1,0:T(8,128)(2,1)S(1)}, u32[]{:S(2)}, u32[]{:S(2)}) collective-permute-start(bf16[512,128]{1,0:T(8,128)(2,1)S(1)} %bitcast.14), channel_id=1, source_target_pairs={{8,4},{12,8},{9,5},{13,9},{10,6},{14,10},{11,7},{15,11},{24,20},{2... | collective-permute-start | bytes 393224 | tf_op jit(solution)/shard_map/ppermute | solution.py:27
  20.2 0.0 collective-permute-done.3
  20.2 0.0 collective-permute-done.5
  20.2 0.1 shard_map.88
  20.3 0.7 %collective-permute-start.6 = (bf16[512,128]{1,0:T(8,128)(2,1)S(1)}, bf16[512,128]{1,0:T(8,128)(2,1)S(1)}, u32[]{:S(2)}, u32[]{:S(2)}) collective-permute-start(bf16[512,128]{1,0:T(8,128)(2,1)S(1)} %bitcast.15), channel_id=1, source_target_pairs={{8,4},{12,8},{9,5},{13,9},{10,6},{14,10},{11,7},{15,11},{24,20},{2... | collective-permute-start | bytes 393224 | tf_op jit(solution)/shard_map/ppermute | solution.py:27
  21.0 0.6 %shard_map.89 = (f32[512,128]{1,0:T(8,128)S(1)}, bf16[4,128,1024]{2,1,0:T(8,128)(2,1)S(1)}) custom-call(bf16[4,128,1024]{2,1,0:T(8,128)(2,1)S(1)} %get-tuple-element.30.dot_ref, f32[4,8,1024]{2,1,0:T(8,128)S(1)} %get-tuple-element.38.fin_ref, bf16[896,1024]{1,0:T(8,128)(2,1)S(1)} %get-tuple-element.40.p_ref), custom_call_target="tpu_custom_call" | custom-call | flops 234881024 | bytes 2097152 | tf_op jit(solution)/shard_map/pallas_call | solution.py:428
  21.7 1.2 %shard_map.90 = (f32[512,128]{1,0:T(8,128)S(1)}, bf16[896,1024]{1,0:T(8,128)(2,1)S(1)}) custom-call(bf16[4,128,1024]{2,1,0:T(8,128)(2,1)S(1)} %get-tuple-element.29.qt_ref, bf16[512,128]{1,0:T(8,128)(2,1)S(1)} %collective-permute-done.4.v_ref, f32[4,8,1024]{2,1,0:T(8,128)S(1)} %get-tuple-element.38.fin_ref, bf16[896,1024]{1,0:T(8,128)(2,1)S(1)} %get-tuple-element.40.p_ref, ...), custom_call_target="tpu_custom_call" | custom-call | flops 469762048 | bytes 2097152 | tf_op jit(solution)/shard_map/pallas_call | solution.py:428
  22.9 0.0 collective-permute-done.8
  23.0 1.3 %collective-permute-start.9 = (bf16[512,128]{1,0:T(8,128)(2,1)S(1)}, bf16[512,128]{1,0:T(8,128)(2,1)S(1)}, u32[]{:S(2)}, u32[]{:S(2)}) collective-permute-start(bf16[512,128]{1,0:T(8,128)(2,1)S(1)} %add_convert_fusion), channel_id=1, source_target_pairs={{4,0},{8,4},{12,8},{5,1},{9,5},{13,9},{6,2},{10,6},{14,10},{7,3},{... | collective-permute-start | bytes 393224 | tf_op jit(solution)/shard_map/ppermute | solution.py:27
  24.3 0.0 collective-permute-done.6
  24.3 1.3 %collective-permute-start.7 = (bf16[512,128]{1,0:T(8,128)(2,1)S(1)}, bf16[512,128]{1,0:T(8,128)(2,1)S(1)}, u32[]{:S(2)}, u32[]{:S(2)}) collective-permute-start(bf16[512,128]{1,0:T(8,128)(2,1)S(1)} %add_convert_fusion.1), channel_id=1, source_target_pairs={{4,0},{8,4},{12,8},{5,1},{9,5},{13,9},{6,2},{10,6},{14,10},{7,3},{... | collective-permute-start | bytes 393224 | tf_op jit(solution)/shard_map/ppermute | solution.py:27
  25.6 4.3 %shard_map.91 = (f32[512,128]{1,0:T(8,128)S(1)}, f32[512,128]{1,0:T(8,128)S(1)}, bf16[8,512,128]{2,1,0:T(8,128)(2,1)}, bf16[8,512,128]{2,1,0:T(8,128)(2,1)}) custom-call(bf16[4,128,1024]{2,1,0:T(8,128)(2,1)S(1)} %get-tuple-element.29.qt_ref, bf16[4,128,1024]{2,1,0:T(8,128)(2,1)S(1)} %get-tuple-element.30.dot_ref, bf16[512,128]{1,0:T(8,128)(2,1)S(1)} %bitcast.10, ...), custom_call_target="tpu_custom_call" | custom-call | flops 1509949440 | bytes 2097152 | tf_op jit(solution)/shard_map/pallas_call | solution.py:428
  29.9 5.2 %collective-permute-done.9.vg_ref = bf16[512,128]{1,0:T(8,128)(2,1)S(1)} collective-permute-done((bf16[512,128]{1,0:T(8,128)(2,1)S(1)}, bf16[512,128]{1,0:T(8,128)(2,1)S(1)}, u32[]{:S(2)}, u32[]{:S(2)}) %collective-permute-start.9) | collective-permute-done | bytes 131104 | tf_op jit(solution)/shard_map/ppermute | solution.py:27
  35.1 2.7 %collective-permute-done.7.kg_ref = bf16[512,128]{1,0:T(8,128)(2,1)S(1)} collective-permute-done((bf16[512,128]{1,0:T(8,128)(2,1)S(1)}, bf16[512,128]{1,0:T(8,128)(2,1)S(1)}, u32[]{:S(2)}, u32[]{:S(2)}) %collective-permute-start.7) | collective-permute-done | bytes 131104 | tf_op jit(solution)/shard_map/ppermute | solution.py:27
  37.9 0.7 %shard_map.92 = (bf16[1,512,128]{2,1,0:T(8,128)(2,1)}, bf16[1,512,128]{2,1,0:T(8,128)(2,1)}) custom-call(f32[512,128]{1,0:T(8,128)S(1)} %get-tuple-element.46.dk_ref, f32[512,128]{1,0:T(8,128)S(1)} %get-tuple-element.47.dv_ref, bf16[512,128]{1,0:T(8,128)(2,1)S(1)} %collective-permute-done.7.kg_ref, bf16[512,128]{1,0:T(8,128)(2,1)S(1)} %collective-permute-done.9.vg_ref), custom_call_target="tpu_custom_call" | custom-call | flops 33554432 | bytes 2097152 | tf_op jit(solution)/shard_map/pallas_call | solution.py:428
  (5 shorter events, 0.2 us)
Async XLA Ops:
  0.6 12.9 %collective-permute-start = (bf16[512,128]{1,0:T(8,128)(2,1)}, bf16[512,128]{1,0:T(8,128)(2,1)S(1)}, u32[]{:S(2)}, u32[]{:S(2)}) collective-permute-start(bf16[512,128]{1,0:T(8,128)(2,1)} %bitcast.8), channel_id=1, source_target_pairs={{0,4},{4,8},{8,12},{1,5},{5,9},{9,13},{2,6},{6,10},{10,14},{3,7},{... | collective-permute-start | bytes 393224 | tf_op jit(solution)/shard_map/ppermute | solution.py:27
  5.6 13.7 %collective-permute-start.1 = (bf16[512,128]{1,0:T(8,128)(2,1)}, bf16[512,128]{1,0:T(8,128)(2,1)S(1)}, u32[]{:S(2)}, u32[]{:S(2)}) collective-permute-start(bf16[512,128]{1,0:T(8,128)(2,1)} %bitcast.9), channel_id=1, source_target_pairs={{0,8},{1,9},{2,10},{3,11},{16,24},{17,25},{18,26},{19,27}} | collective-permute-start | bytes 393224 | tf_op jit(solution)/shard_map/ppermute | solution.py:32
  10.1 4.1 %copy-start = (bf16[8,512,128]{2,1,0:T(8,128)(2,1)S(1)}, bf16[8,512,128]{2,1,0:T(8,128)(2,1)}, u32[]{:S(2)}) copy-start(bf16[8,512,128]{2,1,0:T(8,128)(2,1)} %q_ref.5) | copy-start | bytes 3145732
  10.1 4.1 %copy-start.1 = (bf16[8,512,128]{2,1,0:T(8,128)(2,1)S(1)}, bf16[8,512,128]{2,1,0:T(8,128)(2,1)}, u32[]{:S(2)}) copy-start(bf16[8,512,128]{2,1,0:T(8,128)(2,1)} %do_ref.1) | copy-start | bytes 3145732
  10.1 4.1 %copy-start.2 = (bf16[1,512,128]{2,1,0:T(8,128)(2,1)S(1)}, bf16[1,512,128]{2,1,0:T(8,128)(2,1)}, u32[]{:S(2)}) copy-start(bf16[1,512,128]{2,1,0:T(8,128)(2,1)} %k_ref.1) | copy-start | bytes 393220
  10.1 4.1 %copy-start.3 = (bf16[1,512,128]{2,1,0:T(8,128)(2,1)S(1)}, bf16[1,512,128]{2,1,0:T(8,128)(2,1)}, u32[]{:S(2)}) copy-start(bf16[1,512,128]{2,1,0:T(8,128)(2,1)} %v_ref.1) | copy-start | bytes 393220
  10.1 4.1 %copy-start.4 = (s32[4,11]{1,0:T(4,128)S(1)}, s32[4,11]{1,0:T(4,128)}, u32[]{:S(2)}) copy-start(s32[4,11]{1,0:T(4,128)} %link_ref.1) | copy-start | bytes 532
  10.2 6.9 %collective-permute-start.4 = (bf16[512,128]{1,0:T(8,128)(2,1)}, bf16[512,128]{1,0:T(8,128)(2,1)S(1)}, u32[]{:S(2)}, u32[]{:S(2)}) collective-permute-start(bf16[512,128]{1,0:T(8,128)(2,1)} %bitcast.11), channel_id=1, source_target_pairs={{0,4},{4,8},{8,12},{1,5},{5,9},{9,13},{2,6},{6,10},{10,14},{3,7},{... | collective-permute-start | bytes 393224 | tf_op jit(solution)/shard_map/ppermute | solution.py:27
  11.6 8.6 %collective-permute-start.3 = (bf16[512,128]{1,0:T(8,128)(2,1)}, bf16[512,128]{1,0:T(8,128)(2,1)S(1)}, u32[]{:S(2)}, u32[]{:S(2)}) collective-permute-start(bf16[512,128]{1,0:T(8,128)(2,1)} %bitcast.12), channel_id=1, source_target_pairs={{0,8},{1,9},{2,10},{3,11},{16,24},{17,25},{18,26},{19,27}} | collective-permute-start | bytes 393224 | tf_op jit(solution)/shard_map/ppermute | solution.py:32
  13.5 5.8 %collective-permute-start.2 = (bf16[512,128]{1,0:T(8,128)(2,1)S(1)}, bf16[512,128]{1,0:T(8,128)(2,1)S(1)}, u32[]{:S(2)}, u32[]{:S(2)}) collective-permute-start(bf16[512,128]{1,0:T(8,128)(2,1)S(1)} %collective-permute-done.k_ref.kp_ref), channel_id=1, source_target_pairs={{8,12},{9,13},{10,14},{11,15},{24,28},{25,29},{26,30},{27,31}} | collective-permute-start | bytes 393224 | tf_op jit(solution)/shard_map/ppermute | solution.py:33
  17.0 3.2 %collective-permute-start.5 = (bf16[512,128]{1,0:T(8,128)(2,1)S(1)}, bf16[512,128]{1,0:T(8,128)(2,1)S(1)}, u32[]{:S(2)}, u32[]{:S(2)}) collective-permute-start(bf16[512,128]{1,0:T(8,128)(2,1)S(1)} %collective-permute-done.4.v_ref), channel_id=1, source_target_pairs={{8,12},{9,13},{10,14},{11,15},{24,28},{25,29},{26,30},{27,31}} | collective-permute-start | bytes 393224 | tf_op jit(solution)/shard_map/ppermute | solution.py:33
  19.5 3.4 %collective-permute-start.8 = (bf16[512,128]{1,0:T(8,128)(2,1)S(1)}, bf16[512,128]{1,0:T(8,128)(2,1)S(1)}, u32[]{:S(2)}, u32[]{:S(2)}) collective-permute-start(bf16[512,128]{1,0:T(8,128)(2,1)S(1)} %bitcast.14), channel_id=1, source_target_pairs={{8,4},{12,8},{9,5},{13,9},{10,6},{14,10},{11,7},{15,11},{24,20},{2... | collective-permute-start | bytes 393224 | tf_op jit(solution)/shard_map/ppermute | solution.py:27
  20.3 3.9 %collective-permute-start.6 = (bf16[512,128]{1,0:T(8,128)(2,1)S(1)}, bf16[512,128]{1,0:T(8,128)(2,1)S(1)}, u32[]{:S(2)}, u32[]{:S(2)}) collective-permute-start(bf16[512,128]{1,0:T(8,128)(2,1)S(1)} %bitcast.15), channel_id=1, source_target_pairs={{8,4},{12,8},{9,5},{13,9},{10,6},{14,10},{11,7},{15,11},{24,20},{2... | collective-permute-start | bytes 393224 | tf_op jit(solution)/shard_map/ppermute | solution.py:27
  23.0 12.2 %collective-permute-start.9 = (bf16[512,128]{1,0:T(8,128)(2,1)S(1)}, bf16[512,128]{1,0:T(8,128)(2,1)S(1)}, u32[]{:S(2)}, u32[]{:S(2)}) collective-permute-start(bf16[512,128]{1,0:T(8,128)(2,1)S(1)} %add_convert_fusion), channel_id=1, source_target_pairs={{4,0},{8,4},{12,8},{5,1},{9,5},{13,9},{6,2},{10,6},{14,10},{7,3},{... | collective-permute-start | bytes 393224 | tf_op jit(solution)/shard_map/ppermute | solution.py:27
  24.3 13.6 %collective-permute-start.7 = (bf16[512,128]{1,0:T(8,128)(2,1)S(1)}, bf16[512,128]{1,0:T(8,128)(2,1)S(1)}, u32[]{:S(2)}, u32[]{:S(2)}) collective-permute-start(bf16[512,128]{1,0:T(8,128)(2,1)S(1)} %add_convert_fusion.1), channel_id=1, source_target_pairs={{4,0},{8,4},{12,8},{5,1},{9,5},{13,9},{6,2},{10,6},{14,10},{7,3},{... | collective-permute-start | bytes 393224 | tf_op jit(solution)/shard_map/ppermute | solution.py:27

commit v4 on v3

--- a/solution.py
+++ b/solution.py
@@ -139,13 +139,11 @@
     plan, link_ref, causal_ref, q_ref, do_ref, k_ref, v_ref, bias_ref, stat_ref, acc_ref, p_ref, dot_ref, qt_ref
 ):
     first_block = lax.axis_index("ctx") * plan.blocks
-    scalars = []
     for i in range(plan.blocks):
-        scalars.append([])
         for n, (slot_id, offset, _) in enumerate(plan.entries):
-            live = (link_ref[i, slot_id] == 1) & (first_block + i >= offset)
-            scalars[i].append(jnp.where(live, 0.0, NEG).astype(F32))
-            bias_ref[i, n : n + 1, :] = jnp.full((1, plan.lanes), scalars[i][n], F32)
+            dead = jnp.where(link_ref[i : i + 1, slot_id : slot_id + 1] == 1, 0.0, NEG).astype(F32)
+            late = jnp.where(first_block + i >= offset, 0.0, NEG).astype(F32)
+            bias_ref[i, n : n + 1, :] = jnp.broadcast_to(dead + late, (1, plan.lanes))
     values_t = with_ones(v_ref[0].T)
     size = plan.size
 
@@ -157,7 +155,7 @@
     def second(item, raw):
         i, _, lanes = item
         slots = plan.own[i]
-        biases = [scalars[i][n] if plan.entries[n][1] > 0 else None for n, _ in slots]
+        biases = [bias_ref[i, n : n + 1, lanes] if plan.entries[n][1] > 0 else None for n, _ in slots]
         at = plan.own_at[i] * BLK
         exps, top = scores_of(plan, raw, biases, causal_ref[:, lanes], None)
         low = stack([part.astype(BF16) for part in exps])
@@ -420,7 +418,6 @@
         return jax.ShapeDtypeStruct(shape, dtype)
 
     vmem = pl.BlockSpec(memory_space=pltpu.VMEM)
-    smem = pl.BlockSpec(memory_space=pltpu.SMEM)
     hbm = pl.BlockSpec(memory_space=pltpu.HBM)
 
     def call(body, slots, matmuls, outs, operands, scratch=(), places=None, lasts=(), alias=None):
@@ -455,7 +452,7 @@
         local_forward, n_own, 2,
         [bias, stat, acc, own_shape, grads_t, grads_t],
         (link_mask, causal, queries, out_grad, key_rows, value_rows),
-        places=[smem] + [vmem] * 5,
+        places=[vmem] * 6,
     )
     stat_near, acc_near, p_prev = call(
         prev_forward, n_prev, 2,

time: 38.9 us -> 38.9 us (level)
  waiting for transfers between devices: 8.38 us -> 8.81 us
  Pallas kernels: 11.1 us -> 10.7 us
    ppermute x6, waiting for transfers between devices: 8.36 us -> 8.8 us  [shift(): lax.ppermute(value, axis, [(n, n + steps) for n in range(holders, count)...]
    pallas_call x9, Pallas kernels: 11.1 us -> 10.7 us  [call(): pl.pallas_call(functools.partial(body, plan), in_specs=places or [vmem] *...]
  transfers between devices with their start and end apart: 10 -> 10, of which waited for: 3 -> 3; matrix products, arithmetic and copies ran while one was open for 0% -> 0% of each run, Pallas kernels for 27% -> 26%
where the time goes in v4:
time: 38.9 us; the launch traced here: 38.6 us
  starting transfers between devices  18.1 us (47%)
  Pallas kernels  10.7 us (28%)
  waiting for transfers between devices  8.81 us (23%)
  between operations  0.93 us (2%)
    pallas_call x9, Pallas kernels, call(): pl.pallas_call(functools.partial(body, plan), in_specs=places or [vmem] *...  10.7 us
    ppermute x6, starting transfers between devices, shift(): lax.ppermute(value, axis, [(n, n + steps) for n in range(holders, count)...  10.3 us
    ppermute x6, waiting for transfers between devices, shift(): lax.ppermute(value, axis, [(n, n + steps) for n in range(holders, count)...  8.8 us
    ppermute x2, starting transfers between devices, two_up(): lax.ppermute(own, axis, [(n, n + 2) for n in range(0, count - 2, 2)])  6.41 us
    ppermute x2, starting transfers between devices, two_up(): lax.ppermute(near, axis, [(n, n + 1) for n in range(2, count - 1, 2)])  1.33 us
  transfers between devices with their start and end apart: 10, of which 3 were waited for; matrix products, arithmetic and copies ran while one was open for 0% of the time, Pallas kernels for 26%

profile of v4, /device:TPU:0, one launch (start us, length us, event | category | flops | bytes accessed | tf_op | source)
XLA Modules:
  0.0 38.6 jit_solution(14497622708843761057)
XLA Ops:
  0.6 5.0 %collective-permute-start = (bf16[512,128]{1,0:T(8,128)(2,1)}, bf16[512,128]{1,0:T(8,128)(2,1)S(1)}, u32[]{:S(2)}, u32[]{:S(2)}) collective-permute-start(bf16[512,128]{1,0:T(8,128)(2,1)} %bitcast.8), channel_id=1, source_target_pairs={{0,4},{4,8},{8,12},{1,5},{5,9},{9,13},{2,6},{6,10},{10,14},{3,7},{... | collective-permute-start | bytes 393224 | tf_op jit(solution)/shard_map/ppermute | solution.py:27
  5.6 4.5 %collective-permute-start.1 = (bf16[512,128]{1,0:T(8,128)(2,1)}, bf16[512,128]{1,0:T(8,128)(2,1)S(1)}, u32[]{:S(2)}, u32[]{:S(2)}) collective-permute-start(bf16[512,128]{1,0:T(8,128)(2,1)} %bitcast.9), channel_id=1, source_target_pairs={{0,8},{1,9},{2,10},{3,11},{16,24},{17,25},{18,26},{19,27}} | collective-permute-start | bytes 393224 | tf_op jit(solution)/shard_map/ppermute | solution.py:32
  10.1 0.0 copy-start
  10.1 0.0 copy-start.1
  10.1 0.0 copy-start.2
  10.1 0.0 copy-start.3
  10.1 0.0 copy-start.4
  10.2 1.4 %collective-permute-start.4 = (bf16[512,128]{1,0:T(8,128)(2,1)}, bf16[512,128]{1,0:T(8,128)(2,1)S(1)}, u32[]{:S(2)}, u32[]{:S(2)}) collective-permute-start(bf16[512,128]{1,0:T(8,128)(2,1)} %bitcast.11), channel_id=1, source_target_pairs={{0,4},{4,8},{8,12},{1,5},{5,9},{9,13},{2,6},{6,10},{10,14},{3,7},{... | collective-permute-start | bytes 393224 | tf_op jit(solution)/shard_map/ppermute | solution.py:27
  11.6 1.9 %collective-permute-start.3 = (bf16[512,128]{1,0:T(8,128)(2,1)}, bf16[512,128]{1,0:T(8,128)(2,1)S(1)}, u32[]{:S(2)}, u32[]{:S(2)}) collective-permute-start(bf16[512,128]{1,0:T(8,128)(2,1)} %bitcast.12), channel_id=1, source_target_pairs={{0,8},{1,9},{2,10},{3,11},{16,24},{17,25},{18,26},{19,27}} | collective-permute-start | bytes 393224 | tf_op jit(solution)/shard_map/ppermute | solution.py:32
  13.5 0.0 collective-permute-done.k_ref.kp_ref
  13.5 0.7 %collective-permute-start.2 = (bf16[512,128]{1,0:T(8,128)(2,1)S(1)}, bf16[512,128]{1,0:T(8,128)(2,1)S(1)}, u32[]{:S(2)}, u32[]{:S(2)}) collective-permute-start(bf16[512,128]{1,0:T(8,128)(2,1)S(1)} %collective-permute-done.k_ref.kp_ref), channel_id=1, source_target_pairs={{8,12},{9,13},{10,14},{11,15},{24,28},{25,29},{26,30},{27,31}} | collective-permute-start | bytes 393224 | tf_op jit(solution)/shard_map/ppermute | solution.py:33
  14.3 0.0 copy-done
  14.3 0.0 copy-done.1
  14.3 0.0 copy-done.2
  14.3 0.0 copy-done.3
  14.3 0.0 copy-done.4
  14.3 1.9 %shard_map.85 = (f32[4,16,1024]{2,1,0:T(8,128)S(1)}, f32[4,8,1024]{2,1,0:T(8,128)S(1)}, f32[4,136,1024]{2,1,0:T(8,128)S(1)}, bf16[1152,1024]{1,0:T(8,128)(2,1)S(...) custom-call(s32[4,11]{1,0:T(4,128)S(1)} %copy-done.4, f32[128,1024]{1,0:T(8,128)S(1)} %shard_map.84.causal_ref, ...), custom_call_target="tpu_custom_call" | custom-call | flops 603979776 | bytes 2097152 | tf_op jit(solution)/shard_map/pallas_call | solution.py:425
  16.2 0.8 %collective-permute-done.4.v_ref = bf16[512,128]{1,0:T(8,128)(2,1)S(1)} collective-permute-done((bf16[512,128]{1,0:T(8,128)(2,1)}, bf16[512,128]{1,0:T(8,128)(2,1)S(1)}, u32[]{:S(2)}, u32[]{:S(2)}) %collective-permute-start.4) | collective-permute-done | bytes 131104 | tf_op jit(solution)/shard_map/ppermute | solution.py:27
  17.0 0.7 %collective-permute-start.5 = (bf16[512,128]{1,0:T(8,128)(2,1)S(1)}, bf16[512,128]{1,0:T(8,128)(2,1)S(1)}, u32[]{:S(2)}, u32[]{:S(2)}) collective-permute-start(bf16[512,128]{1,0:T(8,128)(2,1)S(1)} %collective-permute-done.4.v_ref), channel_id=1, source_target_pairs={{8,12},{9,13},{10,14},{11,15},{24,28},{25,29},{26,30},{27,31}} | collective-permute-start | bytes 393224 | tf_op jit(solution)/shard_map/ppermute | solution.py:33
  17.7 1.6 %shard_map.86 = (f32[4,8,1024]{2,1,0:T(8,128)S(1)}, f32[4,136,1024]{2,1,0:T(8,128)S(1)}, bf16[896,1024]{1,0:T(8,128)(2,1)S(1)}) custom-call(bf16[8,512,128]{2,1,0:T(8,128)(2,1)S(1)} %copy-done, bf16[512,128]{1,0:T(8,128)(2,1)S(1)} %collective-permute-done.k_ref.kp_ref, bf16[512,128]{1,0:T(8,128)(2,1)S(1)} %collective-permute-done.4.v_ref, ...), custom_call_target="tpu_custom_call" | custom-call | flops 469762048 | bytes 2097152 | tf_op jit(solution)/shard_map/pallas_call | solution.py:425
  19.3 0.0 collective-permute-done.1
  19.4 0.0 collective-permute-done.2
  19.4 0.1 shard_map.87
  19.5 0.7 %collective-permute-start.8 = (bf16[512,128]{1,0:T(8,128)(2,1)S(1)}, bf16[512,128]{1,0:T(8,128)(2,1)S(1)}, u32[]{:S(2)}, u32[]{:S(2)}) collective-permute-start(bf16[512,128]{1,0:T(8,128)(2,1)S(1)} %bitcast.14), channel_id=1, source_target_pairs={{8,4},{12,8},{9,5},{13,9},{10,6},{14,10},{11,7},{15,11},{24,20},{2... | collective-permute-start | bytes 393224 | tf_op jit(solution)/shard_map/ppermute | solution.py:27
  20.2 0.0 collective-permute-done.3
  20.2 0.0 collective-permute-done.5
  20.2 0.1 shard_map.88
  20.3 0.7 %collective-permute-start.6 = (bf16[512,128]{1,0:T(8,128)(2,1)S(1)}, bf16[512,128]{1,0:T(8,128)(2,1)S(1)}, u32[]{:S(2)}, u32[]{:S(2)}) collective-permute-start(bf16[512,128]{1,0:T(8,128)(2,1)S(1)} %bitcast.15), channel_id=1, source_target_pairs={{8,4},{12,8},{9,5},{13,9},{10,6},{14,10},{11,7},{15,11},{24,20},{2... | collective-permute-start | bytes 393224 | tf_op jit(solution)/shard_map/ppermute | solution.py:27
  21.0 0.6 %shard_map.89 = (f32[512,128]{1,0:T(8,128)S(1)}, bf16[4,128,1024]{2,1,0:T(8,128)(2,1)S(1)}) custom-call(bf16[4,128,1024]{2,1,0:T(8,128)(2,1)S(1)} %get-tuple-element.30.dot_ref, f32[4,8,1024]{2,1,0:T(8,128)S(1)} %get-tuple-element.38.fin_ref, bf16[896,1024]{1,0:T(8,128)(2,1)S(1)} %get-tuple-element.40.p_ref), custom_call_target="tpu_custom_call" | custom-call | flops 234881024 | bytes 2097152 | tf_op jit(solution)/shard_map/pallas_call | solution.py:425
  21.7 1.2 %shard_map.90 = (f32[512,128]{1,0:T(8,128)S(1)}, bf16[896,1024]{1,0:T(8,128)(2,1)S(1)}) custom-call(bf16[4,128,1024]{2,1,0:T(8,128)(2,1)S(1)} %get-tuple-element.29.qt_ref, bf16[512,128]{1,0:T(8,128)(2,1)S(1)} %collective-permute-done.4.v_ref, f32[4,8,1024]{2,1,0:T(8,128)S(1)} %get-tuple-element.38.fin_ref, bf16[896,1024]{1,0:T(8,128)(2,1)S(1)} %get-tuple-element.40.p_ref, ...), custom_call_target="tpu_custom_call" | custom-call | flops 469762048 | bytes 2097152 | tf_op jit(solution)/shard_map/pallas_call | solution.py:425
  22.9 0.0 collective-permute-done.8
  23.0 1.3 %collective-permute-start.9 = (bf16[512,128]{1,0:T(8,128)(2,1)S(1)}, bf16[512,128]{1,0:T(8,128)(2,1)S(1)}, u32[]{:S(2)}, u32[]{:S(2)}) collective-permute-start(bf16[512,128]{1,0:T(8,128)(2,1)S(1)} %add_convert_fusion), channel_id=1, source_target_pairs={{4,0},{8,4},{12,8},{5,1},{9,5},{13,9},{6,2},{10,6},{14,10},{7,3},{... | collective-permute-start | bytes 393224 | tf_op jit(solution)/shard_map/ppermute | solution.py:27
  24.3 0.0 collective-permute-done.6
  24.3 1.3 %collective-permute-start.7 = (bf16[512,128]{1,0:T(8,128)(2,1)S(1)}, bf16[512,128]{1,0:T(8,128)(2,1)S(1)}, u32[]{:S(2)}, u32[]{:S(2)}) collective-permute-start(bf16[512,128]{1,0:T(8,128)(2,1)S(1)} %add_convert_fusion.1), channel_id=1, source_target_pairs={{4,0},{8,4},{12,8},{5,1},{9,5},{13,9},{6,2},{10,6},{14,10},{7,3},{... | collective-permute-start | bytes 393224 | tf_op jit(solution)/shard_map/ppermute | solution.py:27
  25.6 4.3 %shard_map.91 = (f32[512,128]{1,0:T(8,128)S(1)}, f32[512,128]{1,0:T(8,128)S(1)}, bf16[8,512,128]{2,1,0:T(8,128)(2,1)}, bf16[8,512,128]{2,1,0:T(8,128)(2,1)}) custom-call(bf16[4,128,1024]{2,1,0:T(8,128)(2,1)S(1)} %get-tuple-element.29.qt_ref, bf16[4,128,1024]{2,1,0:T(8,128)(2,1)S(1)} %get-tuple-element.30.dot_ref, bf16[512,128]{1,0:T(8,128)(2,1)S(1)} %bitcast.10, ...), custom_call_target="tpu_custom_call" | custom-call | flops 1509949440 | bytes 2097152 | tf_op jit(solution)/shard_map/pallas_call | solution.py:425
  29.9 5.2 %collective-permute-done.9.vg_ref = bf16[512,128]{1,0:T(8,128)(2,1)S(1)} collective-permute-done((bf16[512,128]{1,0:T(8,128)(2,1)S(1)}, bf16[512,128]{1,0:T(8,128)(2,1)S(1)}, u32[]{:S(2)}, u32[]{:S(2)}) %collective-permute-start.9) | collective-permute-done | bytes 131104 | tf_op jit(solution)/shard_map/ppermute | solution.py:27
  35.1 2.7 %collective-permute-done.7.kg_ref = bf16[512,128]{1,0:T(8,128)(2,1)S(1)} collective-permute-done((bf16[512,128]{1,0:T(8,128)(2,1)S(1)}, bf16[512,128]{1,0:T(8,128)(2,1)S(1)}, u32[]{:S(2)}, u32[]{:S(2)}) %collective-permute-start.7) | collective-permute-done | bytes 131104 | tf_op jit(solution)/shard_map/ppermute | solution.py:27
  37.9 0.7 %shard_map.92 = (bf16[1,512,128]{2,1,0:T(8,128)(2,1)}, bf16[1,512,128]{2,1,0:T(8,128)(2,1)}) custom-call(f32[512,128]{1,0:T(8,128)S(1)} %get-tuple-element.46.dk_ref, f32[512,128]{1,0:T(8,128)S(1)} %get-tuple-element.47.dv_ref, bf16[512,128]{1,0:T(8,128)(2,1)S(1)} %collective-permute-done.7.kg_ref, bf16[512,128]{1,0:T(8,128)(2,1)S(1)} %collective-permute-done.9.vg_ref), custom_call_target="tpu_custom_call" | custom-call | flops 33554432 | bytes 2097152 | tf_op jit(solution)/shard_map/pallas_call | solution.py:425
  (5 shorter events, 0.2 us)
Async XLA Ops:
  0.6 12.9 %collective-permute-start = (bf16[512,128]{1,0:T(8,128)(2,1)}, bf16[512,128]{1,0:T(8,128)(2,1)S(1)}, u32[]{:S(2)}, u32[]{:S(2)}) collective-permute-start(bf16[512,128]{1,0:T(8,128)(2,1)} %bitcast.8), channel_id=1, source_target_pairs={{0,4},{4,8},{8,12},{1,5},{5,9},{9,13},{2,6},{6,10},{10,14},{3,7},{... | collective-permute-start | bytes 393224 | tf_op jit(solution)/shard_map/ppermute | solution.py:27
  5.6 13.7 %collective-permute-start.1 = (bf16[512,128]{1,0:T(8,128)(2,1)}, bf16[512,128]{1,0:T(8,128)(2,1)S(1)}, u32[]{:S(2)}, u32[]{:S(2)}) collective-permute-start(bf16[512,128]{1,0:T(8,128)(2,1)} %bitcast.9), channel_id=1, source_target_pairs={{0,8},{1,9},{2,10},{3,11},{16,24},{17,25},{18,26},{19,27}} | collective-permute-start | bytes 393224 | tf_op jit(solution)/shard_map/ppermute | solution.py:32
  10.1 4.1 %copy-start = (bf16[8,512,128]{2,1,0:T(8,128)(2,1)S(1)}, bf16[8,512,128]{2,1,0:T(8,128)(2,1)}, u32[]{:S(2)}) copy-start(bf16[8,512,128]{2,1,0:T(8,128)(2,1)} %q_ref.5) | copy-start | bytes 3145732
  10.1 4.1 %copy-start.1 = (bf16[8,512,128]{2,1,0:T(8,128)(2,1)S(1)}, bf16[8,512,128]{2,1,0:T(8,128)(2,1)}, u32[]{:S(2)}) copy-start(bf16[8,512,128]{2,1,0:T(8,128)(2,1)} %do_ref.1) | copy-start | bytes 3145732
  10.1 4.1 %copy-start.2 = (bf16[1,512,128]{2,1,0:T(8,128)(2,1)S(1)}, bf16[1,512,128]{2,1,0:T(8,128)(2,1)}, u32[]{:S(2)}) copy-start(bf16[1,512,128]{2,1,0:T(8,128)(2,1)} %k_ref.1) | copy-start | bytes 393220
  10.1 4.1 %copy-start.3 = (bf16[1,512,128]{2,1,0:T(8,128)(2,1)S(1)}, bf16[1,512,128]{2,1,0:T(8,128)(2,1)}, u32[]{:S(2)}) copy-start(bf16[1,512,128]{2,1,0:T(8,128)(2,1)} %v_ref.1) | copy-start | bytes 393220
  10.1 4.1 %copy-start.4 = (s32[4,11]{1,0:T(4,128)S(1)}, s32[4,11]{1,0:T(4,128)}, u32[]{:S(2)}) copy-start(s32[4,11]{1,0:T(4,128)} %link_ref.1) | copy-start | bytes 532
  10.2 6.9 %collective-permute-start.4 = (bf16[512,128]{1,0:T(8,128)(2,1)}, bf16[512,128]{1,0:T(8,128)(2,1)S(1)}, u32[]{:S(2)}, u32[]{:S(2)}) collective-permute-start(bf16[512,128]{1,0:T(8,128)(2,1)} %bitcast.11), channel_id=1, source_target_pairs={{0,4},{4,8},{8,12},{1,5},{5,9},{9,13},{2,6},{6,10},{10,14},{3,7},{... | collective-permute-start | bytes 393224 | tf_op jit(solution)/shard_map/ppermute | solution.py:27
  11.6 8.6 %collective-permute-start.3 = (bf16[512,128]{1,0:T(8,128)(2,1)}, bf16[512,128]{1,0:T(8,128)(2,1)S(1)}, u32[]{:S(2)}, u32[]{:S(2)}) collective-permute-start(bf16[512,128]{1,0:T(8,128)(2,1)} %bitcast.12), channel_id=1, source_target_pairs={{0,8},{1,9},{2,10},{3,11},{16,24},{17,25},{18,26},{19,27}} | collective-permute-start | bytes 393224 | tf_op jit(solution)/shard_map/ppermute | solution.py:32
  13.5 5.8 %collective-permute-start.2 = (bf16[512,128]{1,0:T(8,128)(2,1)S(1)}, bf16[512,128]{1,0:T(8,128)(2,1)S(1)}, u32[]{:S(2)}, u32[]{:S(2)}) collective-permute-start(bf16[512,128]{1,0:T(8,128)(2,1)S(1)} %collective-permute-done.k_ref.kp_ref), channel_id=1, source_target_pairs={{8,12},{9,13},{10,14},{11,15},{24,28},{25,29},{26,30},{27,31}} | collective-permute-start | bytes 393224 | tf_op jit(solution)/shard_map/ppermute | solution.py:33
  17.0 3.2 %collective-permute-start.5 = (bf16[512,128]{1,0:T(8,128)(2,1)S(1)}, bf16[512,128]{1,0:T(8,128)(2,1)S(1)}, u32[]{:S(2)}, u32[]{:S(2)}) collective-permute-start(bf16[512,128]{1,0:T(8,128)(2,1)S(1)} %collective-permute-done.4.v_ref), channel_id=1, source_target_pairs={{8,12},{9,13},{10,14},{11,15},{24,28},{25,29},{26,30},{27,31}} | collective-permute-start | bytes 393224 | tf_op jit(solution)/shard_map/ppermute | solution.py:33
  19.5 3.4 %collective-permute-start.8 = (bf16[512,128]{1,0:T(8,128)(2,1)S(1)}, bf16[512,128]{1,0:T(8,128)(2,1)S(1)}, u32[]{:S(2)}, u32[]{:S(2)}) collective-permute-start(bf16[512,128]{1,0:T(8,128)(2,1)S(1)} %bitcast.14), channel_id=1, source_target_pairs={{8,4},{12,8},{9,5},{13,9},{10,6},{14,10},{11,7},{15,11},{24,20},{2... | collective-permute-start | bytes 393224 | tf_op jit(solution)/shard_map/ppermute | solution.py:27
  20.3 3.9 %collective-permute-start.6 = (bf16[512,128]{1,0:T(8,128)(2,1)S(1)}, bf16[512,128]{1,0:T(8,128)(2,1)S(1)}, u32[]{:S(2)}, u32[]{:S(2)}) collective-permute-start(bf16[512,128]{1,0:T(8,128)(2,1)S(1)} %bitcast.15), channel_id=1, source_target_pairs={{8,4},{12,8},{9,5},{13,9},{10,6},{14,10},{11,7},{15,11},{24,20},{2... | collective-permute-start | bytes 393224 | tf_op jit(solution)/shard_map/ppermute | solution.py:27
  23.0 12.2 %collective-permute-start.9 = (bf16[512,128]{1,0:T(8,128)(2,1)S(1)}, bf16[512,128]{1,0:T(8,128)(2,1)S(1)}, u32[]{:S(2)}, u32[]{:S(2)}) collective-permute-start(bf16[512,128]{1,0:T(8,128)(2,1)S(1)} %add_convert_fusion), channel_id=1, source_target_pairs={{4,0},{8,4},{12,8},{5,1},{9,5},{13,9},{6,2},{10,6},{14,10},{7,3},{... | collective-permute-start | bytes 393224 | tf_op jit(solution)/shard_map/ppermute | solution.py:27
  24.3 13.6 %collective-permute-start.7 = (bf16[512,128]{1,0:T(8,128)(2,1)S(1)}, bf16[512,128]{1,0:T(8,128)(2,1)S(1)}, u32[]{:S(2)}, u32[]{:S(2)}) collective-permute-start(bf16[512,128]{1,0:T(8,128)(2,1)S(1)} %add_convert_fusion.1), channel_id=1, source_target_pairs={{4,0},{8,4},{12,8},{5,1},{9,5},{13,9},{6,2},{10,6},{14,10},{7,3},{... | collective-permute-start | bytes 393224 | tf_op jit(solution)/shard_map/ppermute | solution.py:27

commit v5 on v4

--- a/solution.py
+++ b/solution.py
@@ -315,32 +315,37 @@
         ds_ref[ds_at : ds_at + tall, lanes] = (p_ref[p_at : p_at + tall, lanes].astype(F32) * shifted).astype(BF16)
 
 
-def prev_values(plan, dot_ref, fin_ref, p_ref, dv_ref, scaled_ref):
-    sums = {}
+def prev_backward(
+    plan, qt_ref, dot_ref, v_ref, vf_ref, fin_ref, acc_ref, low_ref, p_ref, dk_ref, dv_ref, ds_ref, o_hbm, scaled_ref, o_ref, sems
+):
+    size = plan.size
+    copies = []
     for i in range(plan.blocks):
-        scale_rows(plan, i, 1, dot_ref, fin_ref, scaled_ref)
-        part = p_ref[plan.prev_at[i] * BLK : plan.prev_at[i + 1] * BLK, :]
-        add_blocks(sums, plan.prev[i], dot_nt(part, scaled_ref[i]))
-    for b in range(plan.blocks):
-        dv_ref[block(b)] = sums[b]
-
-
-def prev_keys(plan, qt_ref, v_ref, fin_ref, p_ref, scaled_ref, dk_ref, ds_ref):
-    sums = {}
+        vt = stack([vf_ref[f, block(i)] for f in range(len(plan.far))]).T
+        for heads, lanes in plan.chunks(BACK_WIDE):
+            out_t = acc_ref[i, :size, lanes] * fin_ref[i, 1:2, lanes] + dot_nn(vt, low_ref[i, :, lanes])
+            o_ref[heads, block(i)] = out_t.astype(BF16).T.reshape(BACK_WIDE, BLK, size)
+        copies.append(pltpu.make_async_copy(o_ref.at[:, block(i)], o_hbm.at[:, block(i)], sems.at[i]))
+        copies[i].start()
+    dk_sums, dv_sums = {}, {}
     for i in range(plan.blocks):
         slots = plan.prev[i]
         values = stack([v_ref[block(b)] for _, b in slots])
         at, end = plan.prev_at[i] * BLK, plan.prev_at[i + 1] * BLK
+        scale_rows(plan, i, 1, dot_ref, fin_ref, scaled_ref)
         score_grads(plan, i, slots, values, 1, fin_ref, p_ref, at, ds_ref, at, scaled_ref)
-        dk = dot_nt(ds_ref[at:end, :], qt_ref[i])
-        add_blocks(sums, slots, dk)
+        add_blocks(dv_sums, slots, dot_nt(p_ref[at:end, :], scaled_ref[i]))
+        add_blocks(dk_sums, slots, dot_nt(ds_ref[at:end, :], qt_ref[i]))
     for b in range(plan.blocks):
-        dk_ref[block(b)] = sums[b] * plan.inv_root
+        dk_ref[block(b)] = dk_sums[b] * plan.inv_root
+        dv_ref[block(b)] = dv_sums[b]
+    for copy in copies:
+        copy.wait()
 
 
 def local_backward(
-    plan, qt_ref, dot_ref, k_ref, v_ref, kp_ref, kf_ref, vf_ref, fin_ref, acc_ref, low_ref, p_ref, dsp_ref, dsf_ref,
-    dk_ref, dv_ref, o_hbm, dq_hbm, scaled_ref, ds_ref, o_ref, dq_ref, sems,
+    plan, qt_ref, dot_ref, k_ref, v_ref, kp_ref, kf_ref, fin_ref, p_ref, dsp_ref, dsf_ref,
+    dk_ref, dv_ref, dq_hbm, scaled_ref, ds_ref, dq_ref, sems,
 ):
     size = plan.size
     count = len(plan.far)
@@ -350,12 +355,6 @@
         copies.append(pltpu.make_async_copy(source.at[:, block(i)], target.at[:, block(i)], sems.at[len(copies)]))
         copies[-1].start()
 
-    for i in range(plan.blocks):
-        vt = stack([vf_ref[f, block(i)] for f in range(count)]).T
-        for heads, lanes in plan.chunks(BACK_WIDE):
-            out_t = acc_ref[i, :size, lanes] * fin_ref[i, 1:2, lanes] + dot_nn(vt, low_ref[i, :, lanes])
-            o_ref[heads, block(i)] = out_t.astype(BF16).T.reshape(BACK_WIDE, BLK, size)
-        send(o_ref, o_hbm, i)
     dk_sums, dv_sums = {}, {}
     keys_t = k_ref[...].T
     prev_t = kp_ref[...].T
@@ -389,16 +388,11 @@
         copy.wait()
 
 
-def finish(plan, dk_ref, dv_ref, kg_ref, vg_ref, k_hbm, v_hbm, k_out, v_out, sems):
-    copies = []
-    for n, (own, arrived, out, target) in enumerate(
-        ((dv_ref, vg_ref, v_out, v_hbm), (dk_ref, kg_ref, k_out, k_hbm))
-    ):
-        out[0] = (own[...] + arrived[...].astype(F32)).astype(BF16)
-        copies.append(pltpu.make_async_copy(out, target, sems.at[n]))
-        copies[n].start()
-    for copy in copies:
-        copy.wait()
+def finish(plan, own_ref, arrived_ref, target_hbm, out, sem):
+    out[0] = (own_ref[...] + arrived_ref[...].astype(F32)).astype(BF16)
+    copy = pltpu.make_async_copy(out, target_hbm, sem.at[0])
+    copy.start()
+    copy.wait()
 
 
 def local(queries, key_rows, value_rows, out_grad, link_mask):
@@ -469,16 +463,21 @@
         [far_shape, ds_shape, stat],
         (query_t, grad_t, v_far, low_far, fin),
     )
-    dv_prev, scaled = call(prev_values, n_prev, 1, [total, grads_t], (grad_t, fin, p_prev))
-    dk_prev, ds_prev = call(prev_keys, n_prev, 2, [total, prev_shape], (query_t, v_prev, fin, p_prev, scaled))
-    dk_own, dv_own, output, query_grad = call(
+    dk_prev, dv_prev, ds_prev, output = call(
+        prev_backward, n_prev, 4,
+        [total, total, prev_shape, full],
+        (query_t, grad_t, v_prev, v_far, fin, acc_near, low_far, p_prev),
+        scratch=[pltpu.VMEM(grads_t.shape, BF16), whole, pltpu.SemaphoreType.DMA((blocks,))],
+        lasts=(hbm,),
+    )
+    dk_own, dv_own, query_grad = call(
         local_backward, n_own, 5,
-        [total, total, full, full],
-        (query_t, grad_t, keys, values, k_prev, k_far, v_far, fin, acc_near, low_far, p_own, ds_prev, ds_far),
+        [total, total, full],
+        (query_t, grad_t, keys, values, k_prev, k_far, fin, p_own, ds_prev, ds_far),
         scratch=[
-            pltpu.VMEM(grads_t.shape, BF16), pltpu.VMEM(own_shape.shape, BF16), whole, whole, pltpu.SemaphoreType.DMA((2 * blocks,))
+            pltpu.VMEM(grads_t.shape, BF16), pltpu.VMEM(own_shape.shape, BF16), whole, pltpu.SemaphoreType.DMA((blocks,))
         ],
-        lasts=(hbm, hbm),
+        lasts=(hbm,),
     )
 
     def send_back(pending, prev):
@@ -494,10 +493,12 @@
     v_arrived = send_back(dv_far, dv_prev)
     k_arrived = send_back(dk_far, dk_prev)
     line = array(1, rows, size)
-    key_grad, value_grad = call(
-        finish, 1, 1, [line, line], (dk_own, dv_own, k_arrived, v_arrived),
-        scratch=[pltpu.VMEM(line.shape, BF16), pltpu.VMEM(line.shape, BF16), pltpu.SemaphoreType.DMA((2,))],
-        lasts=(hbm, hbm),
+    value_grad, key_grad = (
+        call(
+            finish, 1, 1, [line], pair,
+            scratch=[pltpu.VMEM(line.shape, BF16), pltpu.SemaphoreType.DMA((1,))], lasts=(hbm,),
+        )[0]
+        for pair in ((dv_own, v_arrived), (dk_own, k_arrived))
     )
     return output, query_grad, key_grad, value_grad
 

time: 38.9 us -> 42.7 us (1.098)
  waiting for transfers between devices: 8.81 us -> 12 us
  Pallas kernels: 10.7 us -> 11.8 us
  starting transfers between devices: 18.1 us -> 17.4 us
    ppermute x6, waiting for transfers between devices: 8.8 us -> 12 us  [shift(): lax.ppermute(value, axis, [(n, n + steps) for n in range(holders, count)...]
    pallas_call x9, Pallas kernels: 10.7 us -> 11.8 us  [call(): pl.pallas_call(functools.partial(body, plan), in_specs=places or [vmem] *...]
    ppermute x2, starting transfers between devices: 6.41 us -> 5.93 us  [two_up(): lax.ppermute(own, axis, [(n, n + 2) for n in range(0, count - 2, 2)])]
where the time goes in v5:
time: 42.7 us; the launch traced here: 42.3 us
  starting transfers between devices  17.4 us (41%)
  waiting for transfers between devices  12 us (28%)
  Pallas kernels  11.8 us (28%)
  between operations  0.94 us (2%)
    ppermute x6, waiting for transfers between devices, shift(): lax.ppermute(value, axis, [(n, n + steps) for n in range(holders, count)...  12 us
    pallas_call x9, Pallas kernels, call(): pl.pallas_call(functools.partial(body, plan), in_specs=places or [vmem] *...  11.8 us
    ppermute x6, starting transfers between devices, shift(): lax.ppermute(value, axis, [(n, n + steps) for n in range(holders, count)...  10.2 us
    ppermute x2, starting transfers between devices, two_up(): lax.ppermute(own, axis, [(n, n + 2) for n in range(0, count - 2, 2)])  5.93 us
    ppermute x2, starting transfers between devices, two_up(): lax.ppermute(near, axis, [(n, n + 1) for n in range(2, count - 1, 2)])  1.33 us
  transfers between devices with their start and end apart: 10, of which 3 were waited for; matrix products, arithmetic and copies ran while one was open for 0% of the time, Pallas kernels for 26%

profile of v5, /device:TPU:0, one launch (start us, length us, event | category | flops | bytes accessed | tf_op | source)
XLA Modules:
  0.0 42.3 jit_solution(1161574234762537243)
XLA Ops:
  0.6 5.0 %collective-permute-start.4 = (bf16[512,128]{1,0:T(8,128)(2,1)}, bf16[512,128]{1,0:T(8,128)(2,1)S(1)}, u32[]{:S(2)}, u32[]{:S(2)}) collective-permute-start(bf16[512,128]{1,0:T(8,128)(2,1)} %bitcast.8), channel_id=1, source_target_pairs={{0,4},{4,8},{8,12},{1,5},{5,9},{9,13},{2,6},{6,10},{10,14},{3,7},{... | collective-permute-start | bytes 393224 | tf_op jit(solution)/shard_map/ppermute | solution.py:27
  5.6 4.5 %collective-permute-start.3 = (bf16[512,128]{1,0:T(8,128)(2,1)}, bf16[512,128]{1,0:T(8,128)(2,1)S(1)}, u32[]{:S(2)}, u32[]{:S(2)}) collective-permute-start(bf16[512,128]{1,0:T(8,128)(2,1)} %bitcast.9), channel_id=1, source_target_pairs={{0,8},{1,9},{2,10},{3,11},{16,24},{17,25},{18,26},{19,27}} | collective-permute-start | bytes 393224 | tf_op jit(solution)/shard_map/ppermute | solution.py:32
  10.1 0.0 copy-start
  10.1 0.0 copy-start.1
  10.1 0.0 copy-start.2
  10.1 0.0 copy-start.3
  10.1 0.0 copy-start.4
  10.2 1.4 %collective-permute-start.1 = (bf16[512,128]{1,0:T(8,128)(2,1)}, bf16[512,128]{1,0:T(8,128)(2,1)S(1)}, u32[]{:S(2)}, u32[]{:S(2)}) collective-permute-start(bf16[512,128]{1,0:T(8,128)(2,1)} %bitcast.11), channel_id=1, source_target_pairs={{0,8},{1,9},{2,10},{3,11},{16,24},{17,25},{18,26},{19,27}} | collective-permute-start | bytes 393224 | tf_op jit(solution)/shard_map/ppermute | solution.py:32
  11.6 1.3 %collective-permute-start = (bf16[512,128]{1,0:T(8,128)(2,1)}, bf16[512,128]{1,0:T(8,128)(2,1)S(1)}, u32[]{:S(2)}, u32[]{:S(2)}) collective-permute-start(bf16[512,128]{1,0:T(8,128)(2,1)} %bitcast.12), channel_id=1, source_target_pairs={{0,4},{4,8},{8,12},{1,5},{5,9},{9,13},{2,6},{6,10},{10,14},{3,7},{... | collective-permute-start | bytes 393224 | tf_op jit(solution)/shard_map/ppermute | solution.py:27
  12.9 0.0 collective-permute-done.4.k_ref.kp_ref
  12.9 0.7 %collective-permute-start.5 = (bf16[512,128]{1,0:T(8,128)(2,1)S(1)}, bf16[512,128]{1,0:T(8,128)(2,1)S(1)}, u32[]{:S(2)}, u32[]{:S(2)}) collective-permute-start(bf16[512,128]{1,0:T(8,128)(2,1)S(1)} %collective-permute-done.4.k_ref.kp_ref), channel_id=1, source_target_pairs={{8,12},{9,13},{10,14},{11,15},{24,28},{25,29},{26,30},{27,31}} | collective-permute-start | bytes 393224 | tf_op jit(solution)/shard_map/ppermute | solution.py:33
  13.6 0.0 copy-done
  13.6 0.0 copy-done.1
  13.7 0.0 copy-done.2
  13.7 0.0 copy-done.3
  13.7 0.0 copy-done.4
  13.7 1.9 %shard_map.85 = (f32[4,16,1024]{2,1,0:T(8,128)S(1)}, f32[4,8,1024]{2,1,0:T(8,128)S(1)}, f32[4,136,1024]{2,1,0:T(8,128)S(1)}, bf16[1152,1024]{1,0:T(8,128)(2,1)S(...) custom-call(s32[4,11]{1,0:T(4,128)S(1)} %copy-done.4, f32[128,1024]{1,0:T(8,128)S(1)} %shard_map.84.causal_ref, ...), custom_call_target="tpu_custom_call" | custom-call | flops 603979776 | bytes 2097152 | tf_op jit(solution)/shard_map/pallas_call | solution.py:419
  15.6 3.0 %collective-permute-done.v_ref = bf16[512,128]{1,0:T(8,128)(2,1)S(1)} collective-permute-done((bf16[512,128]{1,0:T(8,128)(2,1)}, bf16[512,128]{1,0:T(8,128)(2,1)S(1)}, u32[]{:S(2)}, u32[]{:S(2)}) %collective-permute-start) | collective-permute-done | bytes 131104 | tf_op jit(solution)/shard_map/ppermute | solution.py:27
  18.5 0.7 %collective-permute-start.2 = (bf16[512,128]{1,0:T(8,128)(2,1)S(1)}, bf16[512,128]{1,0:T(8,128)(2,1)S(1)}, u32[]{:S(2)}, u32[]{:S(2)}) collective-permute-start(bf16[512,128]{1,0:T(8,128)(2,1)S(1)} %collective-permute-done.v_ref), channel_id=1, source_target_pairs={{8,12},{9,13},{10,14},{11,15},{24,28},{25,29},{26,30},{27,31}} | collective-permute-start | bytes 393224 | tf_op jit(solution)/shard_map/ppermute | solution.py:33
  19.2 1.7 %shard_map.86 = (f32[4,8,1024]{2,1,0:T(8,128)S(1)}, f32[4,136,1024]{2,1,0:T(8,128)S(1)}, bf16[896,1024]{1,0:T(8,128)(2,1)S(1)}) custom-call(bf16[8,512,128]{2,1,0:T(8,128)(2,1)S(1)} %copy-done, bf16[512,128]{1,0:T(8,128)(2,1)S(1)} %collective-permute-done.4.k_ref.kp_ref, bf16[512,128]{1,0:T(8,128)(2,1)S(1)} %collective-permute-done.v_ref, ...), custom_call_target="tpu_custom_call" | custom-call | flops 469762048 | bytes 2097152 | tf_op jit(solution)/shard_map/pallas_call | solution.py:419
  20.9 0.0 collective-permute-done.3
  20.9 0.0 collective-permute-done.5
  20.9 0.1 shard_map.87
  21.0 0.0 collective-permute-done.1
  21.0 0.0 collective-permute-done.2
  21.1 0.1 shard_map.88
  21.2 0.7 %collective-permute-start.6 = (bf16[512,128]{1,0:T(8,128)(2,1)S(1)}, bf16[512,128]{1,0:T(8,128)(2,1)S(1)}, u32[]{:S(2)}, u32[]{:S(2)}) collective-permute-start(bf16[512,128]{1,0:T(8,128)(2,1)S(1)} %bitcast.15), channel_id=1, source_target_pairs={{8,4},{12,8},{9,5},{13,9},{10,6},{14,10},{11,7},{15,11},{24,20},{2... | collective-permute-start | bytes 393224 | tf_op jit(solution)/shard_map/ppermute | solution.py:27
  21.9 0.7 %collective-permute-start.8 = (bf16[512,128]{1,0:T(8,128)(2,1)S(1)}, bf16[512,128]{1,0:T(8,128)(2,1)S(1)}, u32[]{:S(2)}, u32[]{:S(2)}) collective-permute-start(bf16[512,128]{1,0:T(8,128)(2,1)S(1)} %bitcast.14), channel_id=1, source_target_pairs={{8,4},{12,8},{9,5},{13,9},{10,6},{14,10},{11,7},{15,11},{24,20},{2... | collective-permute-start | bytes 393224 | tf_op jit(solution)/shard_map/ppermute | solution.py:27
  22.5 2.9 %shard_map.89 = (f32[512,128]{1,0:T(8,128)S(1)}, f32[512,128]{1,0:T(8,128)S(1)}, bf16[896,1024]{1,0:T(8,128)(2,1)S(1)}, bf16[8,512,128]{2,1,0:T(8,128)(2,1)}) custom-call(bf16[4,128,1024]{2,1,0:T(8,128)(2,1)S(1)} %get-tuple-element.26.qt_ref, bf16[4,128,1024]{2,1,0:T(8,128)(2,1)S(1)} %get-tuple-element.27.dot_ref, ...), custom_call_target="tpu_custom_call" | custom-call | flops 939524096 | bytes 2097152 | tf_op jit(solution)/shard_map/pallas_call | solution.py:419
  25.4 0.0 collective-permute-done.6
  25.5 1.3 %collective-permute-start.7 = (bf16[512,128]{1,0:T(8,128)(2,1)S(1)}, bf16[512,128]{1,0:T(8,128)(2,1)S(1)}, u32[]{:S(2)}, u32[]{:S(2)}) collective-permute-start(bf16[512,128]{1,0:T(8,128)(2,1)S(1)} %add_convert_fusion.1), channel_id=1, source_target_pairs={{4,0},{8,4},{12,8},{5,1},{9,5},{13,9},{6,2},{10,6},{14,10},{7,3},{... | collective-permute-start | bytes 393224 | tf_op jit(solution)/shard_map/ppermute | solution.py:27
  26.8 0.0 collective-permute-done.8
  26.8 1.3 %collective-permute-start.9 = (bf16[512,128]{1,0:T(8,128)(2,1)S(1)}, bf16[512,128]{1,0:T(8,128)(2,1)S(1)}, u32[]{:S(2)}, u32[]{:S(2)}) collective-permute-start(bf16[512,128]{1,0:T(8,128)(2,1)S(1)} %add_convert_fusion), channel_id=1, source_target_pairs={{4,0},{8,4},{12,8},{5,1},{9,5},{13,9},{6,2},{10,6},{14,10},{7,3},{... | collective-permute-start | bytes 393224 | tf_op jit(solution)/shard_map/ppermute | solution.py:27
  28.1 3.8 %shard_map.90 = (f32[512,128]{1,0:T(8,128)S(1)}, f32[512,128]{1,0:T(8,128)S(1)}, bf16[8,512,128]{2,1,0:T(8,128)(2,1)}) custom-call(bf16[4,128,1024]{2,1,0:T(8,128)(2,1)S(1)} %get-tuple-element.26.qt_ref, bf16[4,128,1024]{2,1,0:T(8,128)(2,1)S(1)} %get-tuple-element.27.dot_ref, bf16[512,128]{1,0:T(8,128)(2,1)S(1)} %bitcast.10, bf16[512,128]{1,0:T(8,128)(2,1)S(1)} %bitcast.13, ...), custom_call_target="tpu_custom_call" | custom-call | flops 1509949440 | bytes 2097152 | tf_op jit(solution)/shard_map/pallas_call | solution.py:419
  31.9 7.8 %collective-permute-done.7.arrived_ref = bf16[512,128]{1,0:T(8,128)(2,1)S(1)} collective-permute-done((bf16[512,128]{1,0:T(8,128)(2,1)S(1)}, bf16[512,128]{1,0:T(8,128)(2,1)S(1)}, u32[]{:S(2)}, u32[]{:S(2)}) %collective-permute-start.7) | collective-permute-done | bytes 131104 | tf_op jit(solution)/shard_map/ppermute | solution.py:27
  39.8 0.7 %shard_map.91 = bf16[1,512,128]{2,1,0:T(8,128)(2,1)} custom-call(f32[512,128]{1,0:T(8,128)S(1)} %get-tuple-element.42.own_ref, bf16[512,128]{1,0:T(8,128)(2,1)S(1)} %collective-permute-done.7.arrived_ref), custom_call_target="tpu_custom_call" | custom-call | flops 33554432 | bytes 2097152 | tf_op jit(solution)/shard_map/pallas_call | solution.py:419
  40.5 1.2 %collective-permute-done.9.arrived_ref = bf16[512,128]{1,0:T(8,128)(2,1)S(1)} collective-permute-done((bf16[512,128]{1,0:T(8,128)(2,1)S(1)}, bf16[512,128]{1,0:T(8,128)(2,1)S(1)}, u32[]{:S(2)}, u32[]{:S(2)}) %collective-permute-start.9) | collective-permute-done | bytes 131104 | tf_op jit(solution)/shard_map/ppermute | solution.py:27
  41.6 0.7 %shard_map.92 = bf16[1,512,128]{2,1,0:T(8,128)(2,1)} custom-call(f32[512,128]{1,0:T(8,128)S(1)} %get-tuple-element.45.own_ref, bf16[512,128]{1,0:T(8,128)(2,1)S(1)} %collective-permute-done.9.arrived_ref), custom_call_target="tpu_custom_call" | custom-call | flops 33554432 | bytes 2097152 | tf_op jit(solution)/shard_map/pallas_call | solution.py:419
  (5 shorter events, 0.1 us)
Async XLA Ops:
  0.6 12.3 %collective-permute-start.4 = (bf16[512,128]{1,0:T(8,128)(2,1)}, bf16[512,128]{1,0:T(8,128)(2,1)S(1)}, u32[]{:S(2)}, u32[]{:S(2)}) collective-permute-start(bf16[512,128]{1,0:T(8,128)(2,1)} %bitcast.8), channel_id=1, source_target_pairs={{0,4},{4,8},{8,12},{1,5},{5,9},{9,13},{2,6},{6,10},{10,14},{3,7},{... | collective-permute-start | bytes 393224 | tf_op jit(solution)/shard_map/ppermute | solution.py:27
  5.6 15.3 %collective-permute-start.3 = (bf16[512,128]{1,0:T(8,128)(2,1)}, bf16[512,128]{1,0:T(8,128)(2,1)S(1)}, u32[]{:S(2)}, u32[]{:S(2)}) collective-permute-start(bf16[512,128]{1,0:T(8,128)(2,1)} %bitcast.9), channel_id=1, source_target_pairs={{0,8},{1,9},{2,10},{3,11},{16,24},{17,25},{18,26},{19,27}} | collective-permute-start | bytes 393224 | tf_op jit(solution)/shard_map/ppermute | solution.py:32
  10.1 3.5 %copy-start = (bf16[8,512,128]{2,1,0:T(8,128)(2,1)S(1)}, bf16[8,512,128]{2,1,0:T(8,128)(2,1)}, u32[]{:S(2)}) copy-start(bf16[8,512,128]{2,1,0:T(8,128)(2,1)} %q_ref.5) | copy-start | bytes 3145732
  10.1 3.5 %copy-start.1 = (bf16[8,512,128]{2,1,0:T(8,128)(2,1)S(1)}, bf16[8,512,128]{2,1,0:T(8,128)(2,1)}, u32[]{:S(2)}) copy-start(bf16[8,512,128]{2,1,0:T(8,128)(2,1)} %do_ref.1) | copy-start | bytes 3145732
  10.1 3.5 %copy-start.2 = (bf16[1,512,128]{2,1,0:T(8,128)(2,1)S(1)}, bf16[1,512,128]{2,1,0:T(8,128)(2,1)}, u32[]{:S(2)}) copy-start(bf16[1,512,128]{2,1,0:T(8,128)(2,1)} %k_ref.1) | copy-start | bytes 393220
  10.1 3.5 %copy-start.3 = (bf16[1,512,128]{2,1,0:T(8,128)(2,1)S(1)}, bf16[1,512,128]{2,1,0:T(8,128)(2,1)}, u32[]{:S(2)}) copy-start(bf16[1,512,128]{2,1,0:T(8,128)(2,1)} %v_ref.1) | copy-start | bytes 393220
  10.1 3.5 %copy-start.4 = (s32[4,11]{1,0:T(4,128)S(1)}, s32[4,11]{1,0:T(4,128)}, u32[]{:S(2)}) copy-start(s32[4,11]{1,0:T(4,128)} %link_ref.1) | copy-start | bytes 532
  10.2 10.9 %collective-permute-start.1 = (bf16[512,128]{1,0:T(8,128)(2,1)}, bf16[512,128]{1,0:T(8,128)(2,1)S(1)}, u32[]{:S(2)}, u32[]{:S(2)}) collective-permute-start(bf16[512,128]{1,0:T(8,128)(2,1)} %bitcast.11), channel_id=1, source_target_pairs={{0,8},{1,9},{2,10},{3,11},{16,24},{17,25},{18,26},{19,27}} | collective-permute-start | bytes 393224 | tf_op jit(solution)/shard_map/ppermute | solution.py:32
  11.6 7.0 %collective-permute-start = (bf16[512,128]{1,0:T(8,128)(2,1)}, bf16[512,128]{1,0:T(8,128)(2,1)S(1)}, u32[]{:S(2)}, u32[]{:S(2)}) collective-permute-start(bf16[512,128]{1,0:T(8,128)(2,1)} %bitcast.12), channel_id=1, source_target_pairs={{0,4},{4,8},{8,12},{1,5},{5,9},{9,13},{2,6},{6,10},{10,14},{3,7},{... | collective-permute-start | bytes 393224 | tf_op jit(solution)/shard_map/ppermute | solution.py:27
  12.9 8.0 %collective-permute-start.5 = (bf16[512,128]{1,0:T(8,128)(2,1)S(1)}, bf16[512,128]{1,0:T(8,128)(2,1)S(1)}, u32[]{:S(2)}, u32[]{:S(2)}) collective-permute-start(bf16[512,128]{1,0:T(8,128)(2,1)S(1)} %collective-permute-done.4.k_ref.kp_ref), channel_id=1, source_target_pairs={{8,12},{9,13},{10,14},{11,15},{24,28},{25,29},{26,30},{27,31}} | collective-permute-start | bytes 393224 | tf_op jit(solution)/shard_map/ppermute | solution.py:33
  18.5 2.5 %collective-permute-start.2 = (bf16[512,128]{1,0:T(8,128)(2,1)S(1)}, bf16[512,128]{1,0:T(8,128)(2,1)S(1)}, u32[]{:S(2)}, u32[]{:S(2)}) collective-permute-start(bf16[512,128]{1,0:T(8,128)(2,1)S(1)} %collective-permute-done.v_ref), channel_id=1, source_target_pairs={{8,12},{9,13},{10,14},{11,15},{24,28},{25,29},{26,30},{27,31}} | collective-permute-start | bytes 393224 | tf_op jit(solution)/shard_map/ppermute | solution.py:33
  21.2 4.2 %collective-permute-start.6 = (bf16[512,128]{1,0:T(8,128)(2,1)S(1)}, bf16[512,128]{1,0:T(8,128)(2,1)S(1)}, u32[]{:S(2)}, u32[]{:S(2)}) collective-permute-start(bf16[512,128]{1,0:T(8,128)(2,1)S(1)} %bitcast.15), channel_id=1, source_target_pairs={{8,4},{12,8},{9,5},{13,9},{10,6},{14,10},{11,7},{15,11},{24,20},{2... | collective-permute-start | bytes 393224 | tf_op jit(solution)/shard_map/ppermute | solution.py:27
  21.9 4.9 %collective-permute-start.8 = (bf16[512,128]{1,0:T(8,128)(2,1)S(1)}, bf16[512,128]{1,0:T(8,128)(2,1)S(1)}, u32[]{:S(2)}, u32[]{:S(2)}) collective-permute-start(bf16[512,128]{1,0:T(8,128)(2,1)S(1)} %bitcast.14), channel_id=1, source_target_pairs={{8,4},{12,8},{9,5},{13,9},{10,6},{14,10},{11,7},{15,11},{24,20},{2... | collective-permute-start | bytes 393224 | tf_op jit(solution)/shard_map/ppermute | solution.py:27
  25.5 14.3 %collective-permute-start.7 = (bf16[512,128]{1,0:T(8,128)(2,1)S(1)}, bf16[512,128]{1,0:T(8,128)(2,1)S(1)}, u32[]{:S(2)}, u32[]{:S(2)}) collective-permute-start(bf16[512,128]{1,0:T(8,128)(2,1)S(1)} %add_convert_fusion.1), channel_id=1, source_target_pairs={{4,0},{8,4},{12,8},{5,1},{9,5},{13,9},{6,2},{10,6},{14,10},{7,3},{... | collective-permute-start | bytes 393224 | tf_op jit(solution)/shard_map/ppermute | solution.py:27
  26.8 14.8 %collective-permute-start.9 = (bf16[512,128]{1,0:T(8,128)(2,1)S(1)}, bf16[512,128]{1,0:T(8,128)(2,1)S(1)}, u32[]{:S(2)}, u32[]{:S(2)}) collective-permute-start(bf16[512,128]{1,0:T(8,128)(2,1)S(1)} %add_convert_fusion), channel_id=1, source_target_pairs={{4,0},{8,4},{12,8},{5,1},{9,5},{13,9},{6,2},{10,6},{14,10},{7,3},{... | collective-permute-start | bytes 393224 | tf_op jit(solution)/shard_map/ppermute | solution.py:27
